TPU v7x, 256 devices: a whole 4x4x8 slice. The times are simulated.
256 devices in a mesh: store: 8 (over y, core), tensor: 32 (over z, x).
Axes of the slice: x: 4, y: 4, z: 8, core: 2. Of those that a mesh axis runs over, the one named last changes fastest.
Arguments:
- decoder_rows: bfloat16 [16384, 4096], P(('store', 'tensor')), may hold values from -45 to 45
- q_weight: bfloat16 [4096, 4096], P(None, 'tensor'), may hold values from -0.09375 to 0.09375
- kv_weight: bfloat16 [2, 896, 4096], P(None, None, 'tensor'), may hold values from -0.1875 to 0.1875
- out_weight: bfloat16 [4096, 4096], P('tensor'), may hold values from -0.5 to 0.5
- store_tiles: bfloat16 [4096, 128, 896], P('store', 'tensor'), may hold values from -6 to 6
- neighbour_shard: int32 [256, 2], replicated, may hold values from 0 to 7, all different within a row; in each aligned block of 32 rows (0 to 31, 32 to 63, ...) at most 12 rows name the same one
- neighbour_tile: int32 [256, 2], replicated, may hold values from 0 to 511
Outputs:
- cross: bfloat16 [16384, 4096], P(('store', 'tensor'))
Inputs may be any that keep to these rules, and one draw needn't show every extreme that they name: `neighbour_shard`: each block's 2 neighbours lie in different shards; among the 32 blocks of one sequence no shard is named more than 12 times, and in some sequence one shard is named exactly 12 times.
All inputs are finite; a program needn't handle non-finite values.
Results may differ from a plain program's by a relative error of at most 0.023.
Values may be sent and summed in bfloat16 or wider, within the bound.
No kernel may reach another device: no remote copies, remote signals or barrier semaphores. Data moves between devices by JAX's collectives and lax.ppermute only.
A program may use at most 128 MiB of HBM per device.

v0:
```python
import math

import jax
import jax.numpy as jnp
from jax import lax
from jax.sharding import PartitionSpec as P

HD = 128
BLOCK = 64
NTOK = 128
NEIGH = 2


def body(
    decoder_rows, q_weight, kv_weight, out_weight, store_tiles, neighbour_shard, neighbour_tile
):
    tensor_count = lax.axis_size("tensor")
    store_count = lax.axis_size("store")
    my_sequence = lax.axis_index("store")
    local_rows = decoder_rows.shape[0]
    seq_len = local_rows * tensor_count
    block_count = seq_len // BLOCK
    request_count = block_count * NEIGH
    capacity = 3 * request_count // (2 * store_count)
    head_cols = q_weight.shape[1]
    head_count = head_cols // HD
    q_factor = 1.0 / math.sqrt(HD)
    rows_wide = decoder_rows.astype(jnp.float32)
    normed = (
        rows_wide * lax.rsqrt(jnp.mean(rows_wide * rows_wide, axis=1, keepdims=True) + 1e-05)
    ).astype(jnp.bfloat16)
    queries = (
        jnp.dot(
            lax.all_gather(normed, "tensor", axis=0, tiled=True),
            q_weight,
            preferred_element_type=jnp.float32,
        )
        * q_factor
    ).astype(jnp.bfloat16)
    shard_table = neighbour_shard.reshape(store_count, request_count)
    tile_table = neighbour_tile.reshape(store_count, request_count)
    positions = jnp.arange(request_count, dtype=jnp.int32)
    before_mask = positions[None, :] < positions[:, None]
    same_shard = shard_table[:, :, None] == shard_table[:, None, :]
    rank_table = jnp.sum((same_shard & before_mask[None]).astype(jnp.int32), axis=2)
    served_here = shard_table == my_sequence
    slot_ids = jnp.arange(capacity, dtype=jnp.int32)
    slot_match = (
        served_here[:, :, None] & (rank_table[:, :, None] == slot_ids[None, None, :])
    ).astype(jnp.int32)
    slot_tile = jnp.sum(slot_match * tile_table[:, :, None], axis=1)
    outgoing = jnp.take(store_tiles, slot_tile.reshape(-1), axis=0)
    arrived = lax.all_to_all(outgoing, "store", split_axis=0, concat_axis=0, tiled=True)
    own_shard = lax.dynamic_index_in_dim(shard_table, my_sequence, 0, keepdims=False)
    own_rank = lax.dynamic_index_in_dim(rank_table, my_sequence, 0, keepdims=False)
    slot_index = own_shard * capacity + own_rank
    projected = jnp.einsum(
        "rne,ced->rncd",
        jnp.take(lax.all_gather(arrived, "tensor", axis=1, tiled=True), slot_index, axis=0),
        kv_weight,
        preferred_element_type=jnp.float32,
    )
    keys_values = projected.astype(jnp.bfloat16)
    keyed = keys_values.reshape(block_count, NEIGH * NTOK, 2, head_count, HD)
    query_blocks = queries.reshape(block_count, BLOCK, head_count, HD)
    scores = jnp.einsum(
        "cqhd,ckhd->chqk", query_blocks, keyed[:, :, 0], preferred_element_type=jnp.float32
    )
    expo_scores = jnp.exp(scores)
    weights = (expo_scores / jnp.sum(expo_scores, axis=3, keepdims=True)).astype(jnp.bfloat16)
    attended = jnp.einsum(
        "chqk,ckhd->cqhd", weights, keyed[:, :, 1], preferred_element_type=jnp.float32
    )
    attended = attended.astype(jnp.bfloat16).reshape(seq_len, head_cols)
    return lax.psum_scatter(
        jnp.dot(attended, out_weight, preferred_element_type=jnp.float32).astype(jnp.bfloat16),
        "tensor",
        scatter_dimension=0,
        tiled=True,
    )


def solution(mesh):
    in_specs = (
        P(("store", "tensor"), None),
        P(None, "tensor"),
        P(None, None, "tensor"),
        P("tensor", None),
        P("store", "tensor", None),
        P(),
        P(),
    )
    out_specs = P(("store", "tensor"), None)
    return jax.shard_map(body, mesh=mesh, in_specs=in_specs, out_specs=out_specs, check_vma=False)
```

profile of v0, /device:TPU:6, one launch (start us, length us, event | category | flops | bytes accessed | tf_op | source)
XLA Modules:
  0.0 624.2 jit_solution(14406171586889492786)
XLA Ops:
  6.5 0.0 copy-start
  6.5 1.4 fusion.12
  8.0 2.0 fusion.13
  9.9 0.0 all-gather.5.cloned.1.call-update
  10.0 0.0 all-gather.3.cloned.1.call-start
  10.0 0.8 copy.26
  10.8 0.1 reshape.146
  11.0 0.8 copy.27
  11.8 0.1 mul.46
  11.9 0.3 convert_reduce_fusion
  12.3 0.3 select_reduce_fusion
  12.5 0.1 copy.28
  12.6 0.1 reshape.148
  12.7 0.1 reshape.147
  12.8 3.2 gather_fusion
  16.1 0.4 broadcast_select_fusion
  16.5 16.4 %all_to_all.5 = bf16[96,4,896]{2,1,0:T(4,128)(2,1)S(1)} all-to-all(bf16[96,4,896]{2,1,0:T(4,128)(2,1)S(1)} %broadcast_select_fusion), channel_id=1, replica_groups=mesh['store'=8,'tensor'=32] {'store'}, dimensions={0} | all-to-all | bytes 1376256 | tf_op jit(solution)/shard_map/all_to_all | solution.py:53
  32.9 0.9 copy.30
  33.8 0.0 all-gather.3.cloned.1.call-update
  33.9 0.2 reduce-scatter.2.cloned.1.call-start
  34.1 117.6 %all-gather.5.cloned.1.call-done = bf16[2048,4096]{1,0:T(8,128)(2,1)} async-done(((bf16[64,4096]{1,0:T(8,128)(2,1)}), bf16[2048,4096]{1,0:T(8,128)(2,1)}) %all-gather.5.cloned.1.call-update) | async-done | bytes 16777232 | tf_op jit(solution)/shard_map/all_gather | solution.py:34
  151.7 8.2 %fusion.8 = bf16[2048,128]{1,0:T(8,128)(2,1)S(1)} fusion(bf16[2048,4096]{1,0:T(8,128)(2,1)} %all-gather.5.cloned.1.call-done, bf16[4096,128]{1,0:T(8,128)(2,1)S(1)} %copy-done.1), kind=kOutput, calls=%fused_computation.10 | convolution fusion | flops 2148007936 | bytes 18350080 | tf_op jit(solution)/shard_map/dot_general | solution.py:33
  160.0 158.3 %all-gather.3.cloned.1.call-done = bf16[96,128,896]{2,0,1:T(8,128)(2,1)} async-done(((bf16[96,4,896]{2,0,1:T(8,128)(2,1)}), bf16[96,128,896]{2,0,1:T(8,128)(2,1)}) %all-gather.3.cloned.1.call-update) | async-done | bytes 22020112 | tf_op jit(solution)/shard_map/all_gather | solution.py:59
  318.2 21.1 %copy.31 = bf16[96,128,896]{2,1,0:T(8,128)(2,1)} copy(bf16[96,128,896]{2,0,1:T(8,128)(2,1)} %all-gather.3.cloned.1.call-done) | data formatting | bytes 44040192 | tf_op jit(solution)/shard_map/all_gather | solution.py:59
  339.4 15.7 %gather_fusion.1 = bf16[64,128,896]{2,1,0:T(8,128)(2,1)} fusion(bf16[96,128,896]{2,1,0:T(8,128)(2,1)} %copy.31, s32[1024]{0:T(1024)S(1)} %pad_clamp_fusion), kind=kCustom, calls=%fused_computation.1 | custom fusion | bytes 29360384 | tf_op jit(solution)/shard_map/jit(_take)/gather | solution.py:59
  355.1 9.8 %fusion.5 = bf16[64,128,2,128]{3,1,2,0:T(8,128)(2,1)S(1)} fusion(bf16[64,128,896]{2,1,0:T(8,128)(2,1)} %gather_fusion.1, pred[64]{0:T(512)(128)(4,1)S(1)} %get-tuple-element.5, bf16[2,896,128]{2,1,0:T(8,128)(2,1)S(1)} %copy-done.2), kind=kOutput, calls=%fused_computation.8 | convolution fusion | flops 3767533568 | bytes 19333184 | tf_op jit(solution)/shard_map/rne,ced->rncd/dot_general | solution.py:57
  364.8 0.3 copy.32
  365.2 0.9 exponential_reduce_fusion
  366.1 0.6 fusion.11
  366.7 8.3 %convolution_convert_fusion = bf16[2048,4096]{1,0:T(8,128)(2,1)} fusion(bf16[2048,128]{1,0:T(8,128)(2,1)S(1)} %bitcast.45, bf16[128,4096]{1,0:T(8,128)(2,1)S(1)} %copy-done), kind=kOutput, calls=%fused_computation.2 | convolution fusion | flops 2155872256 | bytes 18350080 | tf_op jit(solution)/shard_map/dot_general | solution.py:76
  375.0 0.0 reduce-scatter.2.cloned.1.call-update
  375.0 242.6 %reduce-scatter.2.cloned.1.call-done = bf16[64,4096]{1,0:T(8,128)(2,1)} async-done(((bf16[2048,4096]{1,0:T(8,128)(2,1)}), bf16[64,4096]{1,0:T(8,128)(2,1)}) %reduce-scatter.2.cloned.1.call-update) | async-done | bytes 524304 | tf_op jit(solution)/shard_map/reduce_scatter | solution.py:75
  (15 shorter events, 0.1 us)
Async XLA Ops:
  6.5 360.2 %copy-start = (bf16[128,4096]{1,0:T(8,128)(2,1)S(1)}, bf16[128,4096]{1,0:T(8,128)(2,1)}, u32[]{:S(2)}) copy-start(bf16[128,4096]{1,0:T(8,128)(2,1)} %param.10) | copy-start | bytes 3145732
  6.5 145.2 %copy-start.1 = (bf16[4096,128]{1,0:T(8,128)(2,1)S(1)}, bf16[4096,128]{1,0:T(8,128)(2,1)}, u32[]{:S(2)}) copy-start(bf16[4096,128]{1,0:T(8,128)(2,1)} %param.8) | copy-start | bytes 3145732
  6.5 145.2 %all-gather.5.cloned.1.call-start = ((), (), s32[]{:S(2)}) async-start(), calls=%async_computation.3 | async-start | bytes 17301504 | tf_op jit(solution)/shard_map/all_gather | solution.py:34
  10.0 308.3 %all-gather.3.cloned.1.call-start = ((), (), s32[]{:S(2)}) async-start(), calls=%async_computation.2 | async-start | bytes 22708224 | tf_op jit(solution)/shard_map/all_gather | solution.py:59
  33.9 583.8 %reduce-scatter.2.cloned.1.call-start = ((), (), s32[]{:S(2)}) async-start(), calls=%async_computation.4 | async-start | bytes 17301504 | tf_op jit(solution)/shard_map/reduce_scatter | solution.py:75
  339.4 15.7 %copy-start.2 = (bf16[2,896,128]{2,1,0:T(8,128)(2,1)S(1)}, bf16[2,896,128]{2,1,0:T(8,128)(2,1)}, u32[]{:S(2)}) copy-start(bf16[2,896,128]{2,1,0:T(8,128)(2,1)} %param.9) | copy-start | bytes 1376260
Sparse Core Ops, SparseCore 0:
  10.1 141.5 all-gather.4
  154.3 163.8 all-gather.2
  375.2 242.4 reduce-scatter.1
where the time goes:
time: 625 us; the launch traced here: 624 us
  waiting for transfers between devices  519 us (83%)
  local copies, waits for them, and re-layouts  43.4 us (7%)
  matrix products  27.8 us (4%)
  blocking collectives  16.4 us (3%)
  between operations  13.3 us (2%)
    reduce_scatter x1, waiting for transfers between devices, body(): lax.psum_scatter(jnp.dot(attended, out_weight, preferred_element_type=jnp...  243 us
    all_gather x1, waiting for transfers between devices, body(): lax.all_gather(arrived, 'tensor', axis=1, tiled=True)  158 us
    all_gather x1, waiting for transfers between devices, body(): lax.all_gather(normed, 'tensor', axis=0, tiled=True)  118 us
    all_gather x1, local copies, waits for them, and re-layouts, body(): lax.all_gather(arrived, 'tensor', axis=1, tiled=True)  21.1 us
    all_to_all x1, blocking collectives, body(): lax.all_to_all(outgoing, 'store', split_axis=0, concat_axis=0, tiled=True)  16.4 us
    gather x1, local copies, waits for them, and re-layouts, body(): jnp.take(lax.all_gather(arrived, 'tensor', axis=1, tiled=True), slot_inde...  15.7 us
  transfers between devices with their start and end apart: 3, of which 3 were waited for; matrix products, arithmetic and copies ran while one was open for 2% of the time, Pallas kernels for 0%

commit v1 on v0

v1 whole, which is shorter than its diff:
```python
import functools
import math

import jax
import jax.numpy as jnp
from jax import lax
from jax.experimental import pallas as pl
from jax.experimental.pallas import tpu as pltpu
from jax.sharding import Mesh, PartitionSpec as P

HD = 128
BLOCK = 64
NTOK = 128
NEIGH = 2
Y, C, Z, X = 4, 2, 8, 4
ROW_AXES = ("c", "x")
GROUP = C * X
HEADS_HERE = 4
ENC = 896
D = 4096


def ring_pairs():
    up = [(z, (z + 1) % Z) for z in range(Z)]
    down = [(Z + z, Z + (z - 1) % Z) for z in range(Z)]
    return up + down


def first_pairs():
    keep = [(z, z) for z in range(Z)]
    down = [(Z + z, Z + (z - 1) % Z) for z in range(Z)]
    return keep + down


def ring(own):
    held = lax.ppermute(own, ("c", "z"), first_pairs())
    pieces = [held]
    for _ in range(HEADS_HERE - 1):
        held = lax.ppermute(held, ("c", "z"), ring_pairs())
        pieces.append(held)
    return pieces


def attend_kernel(q0, q1, q2, q3, nb, k0, k1, k2, k3, o0, o1, o2, o3, out, wkv, wo):
    @pl.when(pl.program_id(0) == 0)
    def _():
        for h, (kv_h, o_h) in enumerate(((k0, o0), (k1, o1), (k2, o2), (k3, o3))):
            wkv[:, h * HD : (h + 1) * HD] = kv_h[0]
            wkv[:, (HEADS_HERE + h) * HD : (HEADS_HERE + h + 1) * HD] = kv_h[1]
            wo[h * HD : (h + 1) * HD, :] = o_h[...]

    tokens = nb[...].reshape(NEIGH * NTOK, ENC)
    keys_values = jnp.dot(tokens, wkv[...], preferred_element_type=jnp.float32).astype(
        jnp.bfloat16
    )
    parts = []
    for h, q_h in enumerate((q0, q1, q2, q3)):
        keys = keys_values[:, h * HD : (h + 1) * HD]
        values = keys_values[:, (HEADS_HERE + h) * HD : (HEADS_HERE + h + 1) * HD]
        scores = lax.dot_general(
            q_h[...], keys, (((1,), (1,)), ((), ())), preferred_element_type=jnp.float32
        )
        expo = jnp.exp(scores)
        weights = (expo / jnp.sum(expo, axis=1, keepdims=True)).astype(jnp.bfloat16)
        parts.append(
            jnp.dot(weights, values, preferred_element_type=jnp.float32).astype(jnp.bfloat16)
        )
    attended = jnp.concatenate(parts, axis=1)
    for n in range(0, D, 512):
        out[:, n : n + 512] = jnp.dot(
            attended, wo[:, n : n + 512], preferred_element_type=jnp.float32
        ).astype(jnp.bfloat16)


def attend(queries, neighbours, kvs, outs):
    const2 = lambda g: (0, 0)
    const3 = lambda g: (0, 0, 0)
    return pl.pallas_call(
        attend_kernel,
        grid=(GROUP,),
        in_specs=[pl.BlockSpec((BLOCK, HD), lambda g: (g, 0))] * 4
        + [
            pl.BlockSpec(
                (None, X, None, NEIGH, NTOK // X, ENC),
                lambda g: (g // X, 0, g % X, 0, 0, 0),
            )
        ]
        + [pl.BlockSpec((2, ENC, HD), const3)] * 4
        + [pl.BlockSpec((HD, D), const2)] * 4,
        out_specs=pl.BlockSpec((BLOCK, D), lambda g: (g, 0)),
        out_shape=jax.ShapeDtypeStruct((GROUP * BLOCK, D), jnp.bfloat16),
        scratch_shapes=[
            pltpu.VMEM((ENC, 2 * HEADS_HERE * HD), jnp.bfloat16),
            pltpu.VMEM((HEADS_HERE * HD, D), jnp.bfloat16),
        ],
        compiler_params=pltpu.CompilerParams(vmem_limit_bytes=48 << 20),
        cost_estimate=pl.CostEstimate(
            flops=7_000_000_000, bytes_accessed=16_000_000, transcendentals=524_288
        ),
    )(*queries, neighbours, *kvs, *outs)


def body(
    decoder_rows, q_weight, kv_weight, out_weight, store_tiles, neighbour_shard, neighbour_tile
):
    store_count = Y * C
    my_sequence = lax.axis_index(("y", "c"))
    request_count = Z * X * NEIGH
    capacity = 3 * request_count // (2 * store_count)
    q_factor = 1.0 / math.sqrt(HD)

    rows_wide = decoder_rows.astype(jnp.float32)
    normed = (
        rows_wide * lax.rsqrt(jnp.mean(rows_wide * rows_wide, axis=1, keepdims=True) + 1e-05)
    ).astype(jnp.bfloat16)
    rows = lax.all_gather(normed, ROW_AXES, axis=0, tiled=True)

    q_pieces = ring(q_weight)
    kv_pieces = ring(kv_weight)
    out_pieces = ring(out_weight)

    shard_table = neighbour_shard.reshape(store_count, request_count)
    tile_table = neighbour_tile.reshape(store_count, request_count)
    positions = jnp.arange(request_count, dtype=jnp.int32)
    before_mask = positions[None, :] < positions[:, None]
    same_shard = shard_table[:, :, None] == shard_table[:, None, :]
    rank_table = jnp.sum((same_shard & before_mask[None]).astype(jnp.int32), axis=2)
    served_here = shard_table == my_sequence
    slot_ids = jnp.arange(capacity, dtype=jnp.int32)
    slot_match = (
        served_here[:, :, None] & (rank_table[:, :, None] == slot_ids[None, None, :])
    ).astype(jnp.int32)
    slot_tile = jnp.sum(slot_match * tile_table[:, :, None], axis=1)
    outgoing = jnp.take(store_tiles, slot_tile.reshape(-1), axis=0)
    arrived = lax.all_to_all(outgoing, ("y", "c"), split_axis=0, concat_axis=0, tiled=True)
    own_shard = lax.dynamic_index_in_dim(shard_table, my_sequence, 0, keepdims=False)
    own_rank = lax.dynamic_index_in_dim(rank_table, my_sequence, 0, keepdims=False)
    slot_index = own_shard * capacity + own_rank
    wanted = jnp.take(arrived, slot_index, axis=0)
    slices = lax.all_to_all(wanted, "z", split_axis=0, concat_axis=0, tiled=True)
    per_z = X * NEIGH
    own_tokens = store_tiles.shape[1]
    column = (
        slices.reshape(Z, per_z, own_tokens, ENC)
        .transpose(1, 0, 2, 3)
        .reshape(per_z, Z * own_tokens, ENC)
    )
    neighbours = lax.all_gather(column, ROW_AXES, axis=0, tiled=True).reshape(
        C, X, X, NEIGH, Z * own_tokens, ENC
    )

    queries = [
        (jnp.dot(rows, piece, preferred_element_type=jnp.float32) * q_factor).astype(jnp.bfloat16)
        for piece in q_pieces
    ]
    partial = attend(queries, neighbours, kv_pieces, out_pieces)
    return lax.psum_scatter(partial, ROW_AXES, scatter_dimension=0, tiled=True)


def solution(mesh):
    grid = Mesh(mesh.devices.reshape(Y, C, Z, X), ("y", "c", "z", "x"))
    tensor = ("z", "x")
    store = ("y", "c")
    in_specs = (
        P(("y", "c", "z", "x"), None),
        P(None, tensor),
        P(None, None, tensor),
        P(tensor, None),
        P(store, tensor, None),
        P(),
        P(),
    )
    out_specs = P(("y", "c", "z", "x"), None)
    return jax.shard_map(body, mesh=grid, in_specs=in_specs, out_specs=out_specs, check_vma=False)
```

time: 625 us -> 262 us (0.42)
  waiting for transfers between devices: 519 us -> 163 us
  local copies, waits for them, and re-layouts: 43.4 us -> 12 us
  Pallas kernels: 0 us -> 21.3 us
  matrix products: 27.8 us -> 10.7 us
  starting transfers between devices: 0.27 us -> 8.77 us
  blocking collectives: 16.4 us -> 24.2 us
    all_gather x2, waiting for transfers between devices: 276 us -> 0.02 us  [the longest x1 0.02 us: body(): rows = lax.all_gather(normed, ROW_AXES, axis=0, tiled=True)]
    reduce_scatter x1, waiting for transfers between devices: 243 us -> 69.4 us  [body(): return lax.psum_scatter(partial, ROW_AXES, scatter_dimension=0, tiled=True)]
    ppermute x0 -> x12, waiting for transfers between devices: none -> 81.6 us  [the longest x9 81.6 us: ring(): held = lax.ppermute(held, ('c', 'z'), ring_pairs())]
    pallas_call x0 -> x1, Pallas kernels: none -> 21.3 us  [attend(): pl.pallas_call(attend_kernel, grid=(GROUP,), in_specs=[pl.BlockSpec((BLOC...]
    all_gather x1 -> x0, local copies, waits for them, and re-layouts: 21.1 us -> none  [body(): lax.all_gather(arrived, 'tensor', axis=1, tiled=True)]
    dot_general x5 -> x4, matrix products: 27.8 us -> 10.7 us  [body(): jnp.dot(rows, piece, preferred_element_type=jnp.float32) * q_factor]
    gather x1, local copies, waits for them, and re-layouts: 15.7 us -> 0.98 us  [body(): wanted = jnp.take(arrived, slot_index, axis=0)]
    all_to_all x0 -> x1, waiting for transfers between devices: none -> 12 us  [body(): lax.all_to_all(outgoing, ('y', 'c'), split_axis=0, concat_axis=0, tiled=T...]
  transfers between devices with their start and end apart: 3 -> 16, of which waited for: 3 -> 8; matrix products, arithmetic and copies ran while one was open for 2% -> 8% of each run, Pallas kernels for 0% -> 0%
where the time goes in v1:
time: 262 us; the launch traced here: 259 us
  waiting for transfers between devices  163 us (62%)
  blocking collectives  24.2 us (9%)
  Pallas kernels  21.3 us (8%)
  between operations  13.4 us (5%)
  local copies, waits for them, and re-layouts  12 us (5%)
  matrix products  10.7 us (4%)
  starting transfers between devices  8.77 us (3%)
  other arithmetic  5.47 us (2%)
    ppermute x9, waiting for transfers between devices, ring(): held = lax.ppermute(held, ('c', 'z'), ring_pairs())  81.6 us
    reduce_scatter x1, waiting for transfers between devices, body(): return lax.psum_scatter(partial, ROW_AXES, scatter_dimension=0, tiled=True)  69.4 us
    all_to_all x1, blocking collectives, body(): lax.all_to_all(wanted, 'z', split_axis=0, concat_axis=0, tiled=True)  24.2 us
    pallas_call x1, Pallas kernels, attend(): pl.pallas_call(attend_kernel, grid=(GROUP,), in_specs=[pl.BlockSpec((BLOC...  21.3 us
    all_to_all x1, waiting for transfers between devices, body(): lax.all_to_all(outgoing, ('y', 'c'), split_axis=0, concat_axis=0, tiled=T...  12 us
    dot_general x4, matrix products, body(): jnp.dot(rows, piece, preferred_element_type=jnp.float32) * q_factor  10.7 us
    unnamed x24, local copies, waits for them, and re-layouts  6.29 us
  transfers between devices with their start and end apart: 16, of which 8 were waited for; matrix products, arithmetic and copies ran while one was open for 8% of the time, Pallas kernels for 0%

profile of v1, /device:TPU:6, one launch (start us, length us, event | category | flops | bytes accessed | tf_op | source)
XLA Modules:
  0.0 259.0 jit_solution(2635928570718165655)
XLA Ops:
  6.5 1.2 fusion.4
  7.8 2.0 fusion.5
  9.8 0.8 copy.15
  10.8 0.8 copy.16
  12.6 3.2 %gather_fusion = bf16[96,4,896]{2,1,0:T(4,128)(2,1)S(1)} fusion(bf16[512,4,896]{2,1,0:T(4,128)(2,1)} %param.11, s32[1024]{0:T(1024)S(1)} %pad_clamp_fusion.1), kind=kCustom, calls=%fused_computation | custom fusion | bytes 1376640 | tf_op jit(solution)/shard_map/jit(_take)/gather | solution.py:134
  15.9 1.3 broadcast_select_fusion
  17.2 4.5 %all-to-all-start = ((bf16[96,4,896]{2,1,0:T(4,128)(2,1)}), bf16[96,4,896]{2,1,0:T(4,128)(2,1)S(1)}, u32[]{:S(2)}, u32[]{:S(2)}) async-start(bf16[96,4,896]{2,1,0:T(4,128)(2,1)} %broadcast_select_fusion), calls=%async_computation | async-start | bytes 1376256 | tf_op jit(solution)/shard_map/all_to_all | solution.py:135
  21.7 12.0 %all-to-all-done = bf16[96,4,896]{2,1,0:T(4,128)(2,1)S(1)} async-done(((bf16[96,4,896]{2,1,0:T(4,128)(2,1)}), bf16[96,4,896]{2,1,0:T(4,128)(2,1)S(1)}, u32[]{:S(2)}, u32[]{:S(2)}) %all-to-all-start) | async-done | bytes 688160 | tf_op jit(solution)/shard_map/all_to_all | solution.py:135
  33.8 1.0 gather_fusion.1
  35.0 24.2 %all_to_all.10 = bf16[64,4,896]{2,1,0:T(4,128)(2,1)S(1)} all-to-all(bf16[64,4,896]{2,1,0:T(4,128)(2,1)S(1)} %broadcast_select_fusion.1), channel_id=1, replica_groups=mesh['y'=4,'c'=2,'z'=8,'x'=4] {'z'}, dimensions={0} | all-to-all | bytes 917504 | tf_op jit(solution)/shard_map/all_to_all | solution.py:140
  59.4 0.9 reshape.127
  60.3 0.7 collective-permute-start
  61.1 0.7 collective-permute-start.8
  61.8 0.6 collective-permute-start.1
  62.6 1.7 collective-permute-start.4
  64.2 13.7 %collective-permute-done.1 = bf16[4096,128]{1,0:T(8,128)(2,1)S(1)} collective-permute-done((bf16[4096,128]{1,0:T(8,128)(2,1)S(1)}, bf16[4096,128]{1,0:T(8,128)(2,1)S(1)}, u32[]{:S(2)}, u32[]{:S(2)}) %collective-permute-start.1) | collective-permute-done | bytes 1048608 | tf_op jit(solution)/shard_map/ppermute | solution.py:39
  77.9 11.2 %collective-permute-done.9.o1 = bf16[128,4096]{1,0:T(8,128)(2,1)S(1)} collective-permute-done((bf16[128,4096]{1,0:T(8,128)(2,1)S(1)}, bf16[128,4096]{1,0:T(8,128)(2,1)S(1)}, u32[]{:S(2)}, u32[]{:S(2)}) %collective-permute-start.9) | collective-permute-done | bytes 1048608 | tf_op jit(solution)/shard_map/ppermute | solution.py:39
  89.3 0.8 copy-done
  90.0 26.5 %collective-permute-done.5.k1 = bf16[2,896,128]{2,1,0:T(8,128)(2,1)S(1)} collective-permute-done((bf16[2,896,128]{2,1,0:T(8,128)(2,1)S(1)}, bf16[2,896,128]{2,1,0:T(8,128)(2,1)S(1)}, u32[]{:S(2)}, u32[]{:S(2)}) %collective-permute-start.5) | collective-permute-done | bytes 458784 | tf_op jit(solution)/shard_map/ppermute | solution.py:39
  116.5 0.8 copy-done.2
  117.3 9.0 %collective-permute-done.6.k2 = bf16[2,896,128]{2,1,0:T(8,128)(2,1)} collective-permute-done((bf16[2,896,128]{2,1,0:T(8,128)(2,1)S(1)}, bf16[2,896,128]{2,1,0:T(8,128)(2,1)}, u32[]{:S(2)}, u32[]{:S(2)}) %collective-permute-start.6) | collective-permute-done | bytes 458784 | tf_op jit(solution)/shard_map/ppermute | solution.py:39
  126.7 3.9 %fusion.q0 = bf16[512,128]{1,0:T(8,128)(2,1)S(1)} fusion(bf16[512,4096]{1,0:T(8,128)(2,1)} %all-gather.3.cloned.1.call-done, bf16[4096,128]{1,0:T(8,128)(2,1)} %copy-done.8), kind=kOutput, calls=%fused_computation.8 | convolution fusion | flops 537001984 | bytes 5373952 | tf_op jit(solution)/shard_map/dot_general | solution.py:153
  130.7 1.2 fusion.1.q1
  132.0 2.5 fusion.2.q2
  134.5 13.1 %collective-permute-done.3 = bf16[4096,128]{1,0:T(8,128)(2,1)} collective-permute-done((bf16[4096,128]{1,0:T(8,128)(2,1)}, bf16[4096,128]{1,0:T(8,128)(2,1)}, u32[]{:S(2)}, u32[]{:S(2)}) %collective-permute-start.3) | collective-permute-done | bytes 1048608 | tf_op jit(solution)/shard_map/ppermute | solution.py:39
  147.6 3.1 %fusion.3.q3 = bf16[512,128]{1,0:T(8,128)(2,1)} fusion(bf16[512,4096]{1,0:T(8,128)(2,1)S(1)} %copy-done.5, bf16[4096,128]{1,0:T(8,128)(2,1)} %collective-permute-done.3), kind=kOutput, calls=%fused_computation.11 | convolution fusion | flops 537001984 | bytes 5373952 | tf_op jit(solution)/shard_map/dot_general | solution.py:153
  150.7 8.1 %collective-permute-done.11.o3 = bf16[128,4096]{1,0:T(8,128)(2,1)} collective-permute-done((bf16[128,4096]{1,0:T(8,128)(2,1)S(1)}, bf16[128,4096]{1,0:T(8,128)(2,1)}, u32[]{:S(2)}, u32[]{:S(2)}) %collective-permute-start.11) | collective-permute-done | bytes 1048608 | tf_op jit(solution)/shard_map/ppermute | solution.py:39
  158.8 1.0 copy-done.1
  159.8 1.0 copy-done.3
  160.8 0.9 copy-done.4
  161.7 21.3 %shard_map.73 = bf16[512,4096]{1,0:T(8,128)(2,1)} custom-call(bf16[512,128]{1,0:T(8,128)(2,1)S(1)} %fusion.q0, bf16[512,128]{1,0:T(8,128)(2,1)S(1)} %fusion.1.q1, bf16[512,128]{1,0:T(8,128)(2,1)S(1)} %fusion.2.q2, bf16[512,128]{1,0:T(8,128)(2,1)S(1)} %copy-done.4, bf16[2,4,4,2,32,896]{5,4,3,2,1,0:T(8,128)(2,1)} %bitcast.23, ...), custom_call_target="tpu_custom_call" | custom-call | flops 7000000000 | bytes 16000000 | tf_op jit(solution)/shard_map/pallas_call | solution.py:78
  183.1 69.4 %reduce-scatter.2.cloned.1.call-done = bf16[64,4096]{1,0:T(8,128)(2,1)} async-done(((bf16[512,4096]{1,0:T(8,128)(2,1)}), bf16[64,4096]{1,0:T(8,128)(2,1)}) %reduce-scatter.2.cloned.1.call-update) | async-done | bytes 524304 | tf_op jit(solution)/shard_map/reduce_scatter | solution.py:157
  (57 shorter events, 2.4 us)
Async XLA Ops:
  6.5 120.1 %all-gather.3.cloned.1.call-start = ((), (), s32[]{:S(2)}) async-start(), calls=%async_computation.3 | async-start | bytes 4718592 | tf_op jit(solution)/shard_map/all_gather | solution.py:116
  15.9 44.4 %copy-start.6 = (bf16[4096,128]{1,0:T(8,128)(2,1)S(1)}, bf16[4096,128]{1,0:T(8,128)(2,1)}, u32[]{:S(2)}) copy-start(bf16[4096,128]{1,0:T(8,128)(2,1)} %param.8) | copy-start | bytes 3145732
  15.9 45.2 %copy-start.7 = (bf16[128,4096]{1,0:T(8,128)(2,1)S(1)}, bf16[128,4096]{1,0:T(8,128)(2,1)}, u32[]{:S(2)}) copy-start(bf16[128,4096]{1,0:T(8,128)(2,1)} %param.10) | copy-start | bytes 3145732
  17.2 16.6 %all-to-all-start = ((bf16[96,4,896]{2,1,0:T(4,128)(2,1)}), bf16[96,4,896]{2,1,0:T(4,128)(2,1)S(1)}, u32[]{:S(2)}, u32[]{:S(2)}) async-start(bf16[96,4,896]{2,1,0:T(4,128)(2,1)} %broadcast_select_fusion), calls=%async_computation | async-start | bytes 1376256 | tf_op jit(solution)/shard_map/all_to_all | solution.py:135
  21.6 137.2 %all-gather.5.cloned.1.call-start = ((), (), s32[]{:S(2)}) async-start(), calls=%async_computation.4 | async-start | bytes 4128768 | tf_op jit(solution)/shard_map/all_gather | solution.py:148
  60.3 192.2 %reduce-scatter.2.cloned.1.call-start = ((), (), s32[]{:S(2)}) async-start(), calls=%async_computation.5 | async-start | bytes 4718592 | tf_op jit(solution)/shard_map/reduce_scatter | solution.py:157
  60.3 1.5 collective-permute-start
  61.1 1.4 collective-permute-start.8
  61.8 27.3 %copy-start.8 = (bf16[4096,128]{1,0:T(8,128)(2,1)}, bf16[4096,128]{1,0:T(8,128)(2,1)S(1)}, u32[]{:S(2)}) copy-start(bf16[4096,128]{1,0:T(8,128)(2,1)S(1)} %collective-permute-done) | copy-start | bytes 3145732
  61.8 16.1 %collective-permute-start.1 = (bf16[4096,128]{1,0:T(8,128)(2,1)S(1)}, bf16[4096,128]{1,0:T(8,128)(2,1)S(1)}, u32[]{:S(2)}, u32[]{:S(2)}) collective-permute-start(bf16[4096,128]{1,0:T(8,128)(2,1)S(1)} %collective-permute-done), channel_id=1, source_target_pairs={{0,4},{4,8},{8,12},{12,16},{16,20},{20,24},{24,28},{28,0},{32,60},... | collective-permute-start | bytes 3145736 | tf_op jit(solution)/shard_map/ppermute | solution.py:39
  62.5 26.7 %collective-permute-start.9 = (bf16[128,4096]{1,0:T(8,128)(2,1)S(1)}, bf16[128,4096]{1,0:T(8,128)(2,1)S(1)}, u32[]{:S(2)}, u32[]{:S(2)}) collective-permute-start(bf16[128,4096]{1,0:T(8,128)(2,1)S(1)} %collective-permute-done.8.o0), channel_id=1, source_target_pairs={{0,4},{4,8},{8,12},{12,16},{16,20},{20,24},{24,28},{28,0},{32,60},... | collective-permute-start | bytes 3145736 | tf_op jit(solution)/shard_map/ppermute | solution.py:39
  62.6 26.6 %collective-permute-start.4 = (bf16[2,896,128]{2,1,0:T(8,128)(2,1)}, bf16[2,896,128]{2,1,0:T(8,128)(2,1)S(1)}, u32[]{:S(2)}, u32[]{:S(2)}) collective-permute-start(bf16[2,896,128]{2,1,0:T(8,128)(2,1)} %param.9), channel_id=1, source_target_pairs={{0,0},{4,4},{8,8},{12,12},{16,16},{20,20},{24,24},{28,28},{32,60},... | collective-permute-start | bytes 1376264 | tf_op jit(solution)/shard_map/ppermute | solution.py:36
  77.9 48.4 %copy-start.9 = (bf16[4096,128]{1,0:T(8,128)(2,1)}, bf16[4096,128]{1,0:T(8,128)(2,1)S(1)}, u32[]{:S(2)}) copy-start(bf16[4096,128]{1,0:T(8,128)(2,1)S(1)} %collective-permute-done.1) | copy-start | bytes 3145732
  77.9 48.4 %collective-permute-start.2 = (bf16[4096,128]{1,0:T(8,128)(2,1)S(1)}, bf16[4096,128]{1,0:T(8,128)(2,1)}, u32[]{:S(2)}, u32[]{:S(2)}) collective-permute-start(bf16[4096,128]{1,0:T(8,128)(2,1)S(1)} %collective-permute-done.1), channel_id=1, source_target_pairs={{0,4},{4,8},{8,12},{12,16},{16,20},{20,24},{24,28},{28,0},{32,60},... | collective-permute-start | bytes 3145736 | tf_op jit(solution)/shard_map/ppermute | solution.py:39
  89.1 37.2 %collective-permute-start.10 = (bf16[128,4096]{1,0:T(8,128)(2,1)S(1)}, bf16[128,4096]{1,0:T(8,128)(2,1)S(1)}, u32[]{:S(2)}, u32[]{:S(2)}) collective-permute-start(bf16[128,4096]{1,0:T(8,128)(2,1)S(1)} %collective-permute-done.9.o1), channel_id=1, source_target_pairs={{0,4},{4,8},{8,12},{12,16},{16,20},{20,24},{24,28},{28,0},{32,60},... | collective-permute-start | bytes 3145736 | tf_op jit(solution)/shard_map/ppermute | solution.py:39
  89.2 27.4 %collective-permute-start.5 = (bf16[2,896,128]{2,1,0:T(8,128)(2,1)S(1)}, bf16[2,896,128]{2,1,0:T(8,128)(2,1)S(1)}, u32[]{:S(2)}, u32[]{:S(2)}) collective-permute-start(bf16[2,896,128]{2,1,0:T(8,128)(2,1)S(1)} %collective-permute-done.4.k0), channel_id=1, source_target_pairs={{0,4},{4,8},{8,12},{12,16},{16,20},{20,24},{24,28},{28,0},{32,60},... | collective-permute-start | bytes 1376264 | tf_op jit(solution)/shard_map/ppermute | solution.py:39
  89.2 0.8 copy-start
  116.5 9.8 %collective-permute-start.6 = (bf16[2,896,128]{2,1,0:T(8,128)(2,1)S(1)}, bf16[2,896,128]{2,1,0:T(8,128)(2,1)}, u32[]{:S(2)}, u32[]{:S(2)}) collective-permute-start(bf16[2,896,128]{2,1,0:T(8,128)(2,1)S(1)} %collective-permute-done.5.k1), channel_id=1, source_target_pairs={{0,4},{4,8},{8,12},{12,16},{16,20},{20,24},{24,28},{28,0},{32,60},... | collective-permute-start | bytes 1376264 | tf_op jit(solution)/shard_map/ppermute | solution.py:39
  116.5 0.8 copy-start.2
  126.3 24.4 %collective-permute-start.7 = (bf16[2,896,128]{2,1,0:T(8,128)(2,1)}, bf16[2,896,128]{2,1,0:T(8,128)(2,1)}, u32[]{:S(2)}, u32[]{:S(2)}) collective-permute-start(bf16[2,896,128]{2,1,0:T(8,128)(2,1)} %collective-permute-done.6.k2), channel_id=1, source_target_pairs={{0,4},{4,8},{8,12},{12,16},{16,20},{20,24},{24,28},{28,0},{32,60},... | collective-permute-start | bytes 1376264 | tf_op jit(solution)/shard_map/ppermute | solution.py:39
  126.3 21.2 %collective-permute-start.3 = (bf16[4096,128]{1,0:T(8,128)(2,1)}, bf16[4096,128]{1,0:T(8,128)(2,1)}, u32[]{:S(2)}, u32[]{:S(2)}) collective-permute-start(bf16[4096,128]{1,0:T(8,128)(2,1)} %collective-permute-done.2), channel_id=1, source_target_pairs={{0,4},{4,8},{8,12},{12,16},{16,20},{20,24},{24,28},{28,0},{32,60},... | collective-permute-start | bytes 3145736 | tf_op jit(solution)/shard_map/ppermute | solution.py:39
  126.4 32.4 %collective-permute-start.11 = (bf16[128,4096]{1,0:T(8,128)(2,1)S(1)}, bf16[128,4096]{1,0:T(8,128)(2,1)}, u32[]{:S(2)}, u32[]{:S(2)}) collective-permute-start(bf16[128,4096]{1,0:T(8,128)(2,1)S(1)} %collective-permute-done.10.o2), channel_id=1, source_target_pairs={{0,4},{4,8},{8,12},{12,16},{16,20},{20,24},{24,28},{28,0},{32,60},... | collective-permute-start | bytes 3145736 | tf_op jit(solution)/shard_map/ppermute | solution.py:39
  126.7 3.9 %copy-start.5 = (bf16[512,4096]{1,0:T(8,128)(2,1)S(1)}, bf16[512,4096]{1,0:T(8,128)(2,1)}, u32[]{:S(2)}) copy-start(bf16[512,4096]{1,0:T(8,128)(2,1)} %all-gather.3.cloned.1.call-done) | copy-start | bytes 12582916
  126.7 4.0 %copy-start.10 = (bf16[4096,128]{1,0:T(8,128)(2,1)S(1)}, bf16[4096,128]{1,0:T(8,128)(2,1)}, u32[]{:S(2)}) copy-start(bf16[4096,128]{1,0:T(8,128)(2,1)} %copy-done.9) | copy-start | bytes 3145732
  158.8 1.0 copy-start.1
  159.8 1.0 copy-start.3
  160.8 0.9 copy-start.4
Sparse Core Ops, SparseCore 0:
  9.9 35.6 all-gather.2
  60.4 24.9 all-gather.4
  183.2 69.2 reduce-scatter.1

commit v2 on v1

v2 whole, which is shorter than its diff:
```python
import functools
import math

import jax
import jax.numpy as jnp
from jax import lax
from jax.experimental import pallas as pl
from jax.experimental.pallas import tpu as pltpu
from jax.sharding import Mesh, PartitionSpec as P

HD = 128
BLOCK = 64
NTOK = 128
NEIGH = 2
Y, C, Z, X = 4, 2, 8, 4
ROW_AXES = ("c", "x")
GROUP = C * X
HEADS_HERE = 4
ENC = 896
D = 4096


def move(value, pairs):
    return lax.ppermute(value, ("c", "z"), [(c * Z + z, d * Z + w % Z) for c, z, d, w in pairs])


def hop(value, by=1):
    return move(
        value,
        [(0, z, 0, z + by) for z in range(Z)] + [(1, z, 1, z - by) for z in range(Z)],
    )


def last_hop(own, third):
    half = own.shape[0] // 2
    low = move(third[:half], [(1, z, 1, z - 1) for z in range(Z)])
    high = move(third[half:], [(0, z, 1, z + 1) for z in range(Z)])
    return jnp.where(lax.axis_index("c") == 0, own, jnp.concatenate([low, high], axis=0))


def shift(value, axis, by):
    size = lax.axis_size(axis)
    return lax.ppermute(value, axis, [(i, (i + by) % size) for i in range(size)])


def tie(value, *others):
    return lax.optimization_barrier((value, *others))[0]


IN_VMEM = pl.BlockSpec(memory_space=pltpu.VMEM)
IN_SMEM = pl.BlockSpec(memory_space=pltpu.SMEM)


OUT_COLS = D // Y
UNPACK_FLOPS = 18_000_000_000


def unpack_kernel(place, *refs):
    *pieces, wo = refs
    for b in range(2):
        own, up, far0, far1, down = pieces[5 * b : 5 * b + 5]
        for k in range(2):
            row = (2 * b + k) * HD
            for step, piece in enumerate((own.at[k], up.at[k], (far0, far1)[k], down.at[k])):
                quarter = lax.rem(place[2] + step, Y)
                column = pl.multiple_of(quarter * OUT_COLS, OUT_COLS)
                wo[row : row + HD, pl.ds(column, OUT_COLS)] = piece[...]


def unpack(place, pieces):
    return pl.pallas_call(
        unpack_kernel,
        in_specs=[IN_SMEM] + [IN_VMEM] * len(pieces),
        out_specs=IN_VMEM,
        out_shape=jax.ShapeDtypeStruct((HEADS_HERE * HD, D), jnp.bfloat16),
        cost_estimate=pl.CostEstimate(
            flops=UNPACK_FLOPS, bytes_accessed=10_000, transcendentals=0
        ),
    )(place, *pieces)


def attend_kernel(place, q0, q1, q2, q3, kv0, kv1, kv2, kv3, nb, attended, wkv):
    for h, kv in enumerate((kv0, kv1, kv2, kv3)):
        for a in range(2):
            column = (2 * h + a) * HD
            wkv[:, column : column + HD] = kv[a]
    my_c = place[0]
    my_x = place[1]
    for j in range(GROUP):
        if j < C:
            core = lax.rem(my_c + 1 + j, C)
            block = lax.rem(my_x + 2, X)
        else:
            core = lax.rem(my_c + (1 if j < C + X - 1 else 0), C)
            block = lax.rem(my_x + 3 + (j - C) % (X - 1), X)
        tokens = nb[core, :, block].reshape(NEIGH * NTOK, ENC)
        keys_values = jnp.dot(tokens, wkv[...], preferred_element_type=jnp.float32).astype(
            jnp.bfloat16
        )
        first = pl.multiple_of((core * X + block) * BLOCK, BLOCK)
        for h, q_h in enumerate((q0, q1, q2, q3)):
            keys = keys_values[:, 2 * h * HD : (2 * h + 1) * HD]
            values = keys_values[:, (2 * h + 1) * HD : (2 * h + 2) * HD]
            scores = lax.dot_general(
                q_h[pl.ds(first, BLOCK), :],
                keys,
                (((1,), (1,)), ((), ())),
                preferred_element_type=jnp.float32,
            )
            expo = jnp.exp(scores)
            weights = (expo / jnp.sum(expo, axis=1, keepdims=True)).astype(jnp.bfloat16)
            attended[j * BLOCK : (j + 1) * BLOCK, h * HD : (h + 1) * HD] = jnp.dot(
                weights, values, preferred_element_type=jnp.float32
            ).astype(jnp.bfloat16)


def attend(place, queries, kvs, neighbours):
    return pl.pallas_call(
        attend_kernel,
        in_specs=[IN_SMEM] + [IN_VMEM] * (2 * HEADS_HERE + 1),
        out_specs=IN_VMEM,
        out_shape=jax.ShapeDtypeStruct((GROUP * BLOCK, HEADS_HERE * HD), jnp.bfloat16),
        scratch_shapes=[pltpu.VMEM((ENC, 2 * HEADS_HERE * HD), jnp.bfloat16)],
        compiler_params=pltpu.CompilerParams(vmem_limit_bytes=24 << 20),
        cost_estimate=pl.CostEstimate(
            flops=1_000_000, bytes_accessed=10_000, transcendentals=0
        ),
    )(place, *queries, *kvs, neighbours)


def add(*terms):
    return sum(t.astype(jnp.float32) for t in terms).astype(jnp.bfloat16)


def project_and_reduce(attended, wo):
    half = D // 2
    far_end = C * BLOCK
    other_end = far_end + (X - 1) * BLOCK

    def project(first, last):
        rows = jnp.dot(attended[first:last], wo, preferred_element_type=jnp.float32)
        return rows.astype(jnp.bfloat16).reshape(-1, BLOCK, D)

    far = project(0, far_end)
    far_swapped = shift(far[0], "c", 1)
    for_other = project(far_end, other_end)
    swapped = shift(for_other, "c", 1)
    far_sum = add(far[1], far_swapped)
    far_up = shift(far_sum[:, :half], "x", 1)
    far_down = shift(far_sum[:, half:], "x", -1)
    own = project(other_end, GROUP * BLOCK)
    empty = jnp.zeros((BLOCK, half), jnp.bfloat16)
    up_sum = add(own[2], swapped[2], jnp.concatenate([far_up, empty], axis=1))
    down_sum = add(own[0], swapped[0], jnp.concatenate([empty, far_down], axis=1))
    from_below = shift(up_sum, "x", 1)
    from_above = shift(down_sum, "x", -1)
    return add(own[1], swapped[1], from_below, from_above)


def project_queries(rows, weight):
    q_factor = 1.0 / math.sqrt(HD)
    wide = jnp.dot(rows, weight, preferred_element_type=jnp.float32)
    return (wide * q_factor).astype(jnp.bfloat16)


def body(
    decoder_rows, q_weight, kv_weight, out_weight, store_tiles, neighbour_shard, neighbour_tile
):
    store_count = Y * C
    my_sequence = lax.axis_index(("y", "c"))
    request_count = Z * X * NEIGH
    capacity = 3 * request_count // (2 * store_count)

    rows_wide = decoder_rows.astype(jnp.float32)
    normed = (
        rows_wide * lax.rsqrt(jnp.mean(rows_wide * rows_wide, axis=1, keepdims=True) + 1e-05)
    ).astype(jnp.bfloat16)
    rows = lax.all_gather(normed, ROW_AXES, axis=0, tiled=True)

    place = jnp.stack([lax.axis_index(axis) for axis in ("c", "x", "y")]).astype(jnp.int32)
    q_hops = [hop(q_weight)]
    kv_hops = [hop(kv_weight)]
    out_own = lax.dynamic_slice_in_dim(out_weight, place[2] * OUT_COLS, OUT_COLS, axis=1)
    out_near = [hop(out_own), hop(out_own, 2)]

    shard_table = neighbour_shard.reshape(store_count, request_count)
    tile_table = neighbour_tile.reshape(store_count, request_count)
    positions = jnp.arange(request_count, dtype=jnp.int32)
    before_mask = positions[None, :] < positions[:, None]
    same_shard = shard_table[:, :, None] == shard_table[:, None, :]
    rank_table = jnp.sum((same_shard & before_mask[None]).astype(jnp.int32), axis=2)
    served_here = shard_table == my_sequence
    slot_ids = jnp.arange(capacity, dtype=jnp.int32)
    slot_match = (
        served_here[:, :, None] & (rank_table[:, :, None] == slot_ids[None, None, :])
    ).astype(jnp.int32)
    slot_tile = jnp.sum(slot_match * tile_table[:, :, None], axis=1)
    outgoing = jnp.take(store_tiles, slot_tile.reshape(-1), axis=0, mode="clip")
    arrived = lax.all_to_all(outgoing, ("y", "c"), split_axis=0, concat_axis=0, tiled=True)
    own_shard = lax.dynamic_index_in_dim(shard_table, my_sequence, 0, keepdims=False)
    own_rank = lax.dynamic_index_in_dim(rank_table, my_sequence, 0, keepdims=False)
    slot_index = own_shard * capacity + own_rank
    wanted = jnp.take(arrived, slot_index, axis=0, mode="clip")
    wanted, q_first, kv_first, out_first, out_second = lax.optimization_barrier(
        (wanted, q_hops[0], kv_hops[0], *out_near)
    )
    out_pair = jnp.stack([out_first, out_second])
    q_hops.append(hop(q_first))
    kv_hops.append(hop(kv_first))
    out_third = hop(out_first, 2)
    out_fourth = move(out_second, [(1, z, 1, z - 2) for z in range(Z)])
    near_up = shift(out_pair, "y", -1)
    near_down = shift(out_pair, "y", 1)
    queries = [project_queries(rows, q_first)]
    slices = lax.all_to_all(wanted, "z", split_axis=0, concat_axis=0, tiled=True)
    per_z = X * NEIGH
    own_tokens = store_tiles.shape[1]
    column = (
        slices.reshape(Z, per_z, own_tokens, ENC)
        .transpose(1, 0, 2, 3)
        .reshape(per_z, Z * own_tokens, ENC)
    )
    q_second, kv_second = q_hops[1], kv_hops[1]
    q_hops.append(hop(q_second))
    kv_hops.append(hop(kv_second))
    out_last = jnp.where(lax.axis_index("c") == 0, out_own, out_fourth)
    far_pair = jnp.stack([out_third, out_last])
    far_up = shift(far_pair, "y", -1)
    far_down = shift(far_pair, "y", 1)
    near0 = shift(near_up[0], "y", -1)
    near1 = shift(near_down[1], "y", 1)
    queries.append(project_queries(rows, q_second))
    q_third, kv_third = q_hops[2], kv_hops[2]
    q_last = last_hop(q_weight, q_third)
    kv_last = last_hop(kv_weight, kv_third)
    far0 = shift(far_up[0], "y", -1)
    far1 = shift(far_down[1], "y", 1)
    queries.append(project_queries(rows, q_third))
    place_then = tie(place, q_last, kv_last, *queries)
    queries.append(project_queries(rows, q_last))
    kv_pieces = [kv_first, kv_second, kv_third, kv_last]
    wo = unpack(
        place_then,
        (out_pair, near_up, near0, near1, near_down, far_pair, far_up, far0, far1, far_down),
    )
    neighbours = lax.all_gather(column, ROW_AXES, axis=0, tiled=True).reshape(
        C, X, X, NEIGH, Z * own_tokens, ENC
    )

    attended = attend(tie(place, wo), queries, kv_pieces, neighbours)
    return project_and_reduce(attended, wo)


def solution(mesh):
    grid = Mesh(mesh.devices.reshape(Y, C, Z, X), ("y", "c", "z", "x"))
    tensor = ("z", "x")
    store = ("y", "c")
    in_specs = (
        P(("y", "c", "z", "x"), None),
        P(None, tensor),
        P(None, None, tensor),
        P(tensor, None),
        P(store, tensor, None),
        P(),
        P(),
    )
    out_specs = P(("y", "c", "z", "x"), None)
    return jax.shard_map(body, mesh=grid, in_specs=in_specs, out_specs=out_specs, check_vma=False)
```

time: 262 us -> 185 us (0.71)
  waiting for transfers between devices: 163 us -> 47.6 us
  starting transfers between devices: 8.77 us -> 63.9 us
  blocking collectives: 24.2 us -> 0 us
  other arithmetic: 5.47 us -> 11.5 us
  Pallas kernels: 21.3 us -> 15.9 us
  local copies, waits for them, and re-layouts: 12 us -> 17.1 us
  matrix products: 10.7 us -> 14.7 us
    reduce_scatter x1 -> x0, waiting for transfers between devices: 69.4 us -> none  [body(): return lax.psum_scatter(partial, ROW_AXES, scatter_dimension=0, tiled=True)]
    ppermute x12 -> x28, waiting for transfers between devices: 81.6 us -> 28.3 us  [the longest x14 21.1 us: shift(): lax.ppermute(value, axis, [(i, (i + by) % size) for i in range(size)])]
    ppermute x12 -> x28, starting transfers between devices: 4.22 us -> 52.2 us  [the longest x14 31.6 us: move(): lax.ppermute(value, ('c', 'z'), [(c * Z + z, d * Z + w % Z) for c, z, d,...]
    all_to_all x1 -> x0, blocking collectives: 24.2 us -> none  [body(): lax.all_to_all(wanted, 'z', split_axis=0, concat_axis=0, tiled=True)]
    all_to_all x0 -> x1, waiting for transfers between devices: none -> 12.6 us  [body(): lax.all_to_all(wanted, 'z', split_axis=0, concat_axis=0, tiled=True)]
    pallas_call x1 -> x2, Pallas kernels: 21.3 us -> 15.9 us  [the longest x1 11.4 us: attend(): pl.pallas_call(attend_kernel, in_specs=[IN_SMEM] + [IN_VMEM] * (2 * HEADS...]
    all_to_all x1, waiting for transfers between devices: 12 us -> 6.64 us  [body(): lax.all_to_all(outgoing, ('y', 'c'), split_axis=0, concat_axis=0, tiled=T...]
    squeeze x0 -> x4, local copies, waits for them, and re-layouts: none -> 4.87 us  [the longest x1 1.7 us: body(): near1 = shift(near_down[1], 'y', 1)]
  transfers between devices with their start and end apart: 16 -> 32, of which waited for: 8 -> 13; matrix products, arithmetic and copies ran while one was open for 8% -> 19% of each run, Pallas kernels for 0% -> 2%
where the time goes in v2:
time: 185 us
  starting transfers between devices  63.9 us (35%)
  waiting for transfers between devices  47.6 us (26%)
  local copies, waits for them, and re-layouts  17.1 us (9%)
  Pallas kernels  15.9 us (9%)
  matrix products  14.7 us (8%)
  between operations  13.9 us (8%)
  other arithmetic  11.5 us (6%)
    ppermute x14, starting transfers between devices, move(): lax.ppermute(value, ('c', 'z'), [(c * Z + z, d * Z + w % Z) for c, z, d,...  31.6 us
    ppermute x14, waiting for transfers between devices, shift(): lax.ppermute(value, axis, [(i, (i + by) % size) for i in range(size)])  21.1 us
    ppermute x14, starting transfers between devices, shift(): lax.ppermute(value, axis, [(i, (i + by) % size) for i in range(size)])  20.6 us
    all_to_all x1, waiting for transfers between devices, body(): lax.all_to_all(wanted, 'z', split_axis=0, concat_axis=0, tiled=True)  12.6 us
    dot_general x4, matrix products, project_queries(): wide = jnp.dot(rows, weight, preferred_element_type=jnp.float32)  12 us
    pallas_call x1, Pallas kernels, attend(): pl.pallas_call(attend_kernel, in_specs=[IN_SMEM] + [IN_VMEM] * (2 * HEADS...  11.4 us
    all_to_all x1, starting transfers between devices, body(): lax.all_to_all(outgoing, ('y', 'c'), split_axis=0, concat_axis=0, tiled=T...  7.57 us
    ppermute x14, waiting for transfers between devices, move(): lax.ppermute(value, ('c', 'z'), [(c * Z + z, d * Z + w % Z) for c, z, d,...  7.19 us
  transfers between devices with their start and end apart: 32, of which 13 were waited for; matrix products, arithmetic and copies ran while one was open for 19% of the time, Pallas kernels for 2%

profile of v2, /device:TPU:6, one launch (start us, length us, event | category | flops | bytes accessed | tf_op | source)
XLA Modules:
  0.0 184.6 jit_solution(1936696036611093957)
XLA Ops:
  7.9 2.0 %fusion.5 = bf16[64,4096]{1,0:T(8,128)(2,1)} fusion(bf16[64,4096]{1,0:T(8,128)(2,1)} %param.7, f32[64]{0:T(128)S(1)} %add_rsqrt_fusion), kind=kLoop, calls=%fused_computation.16 | loop fusion | flops 786432 | bytes 1048832 | tf_op jit(solution)/shard_map/convert_element_type | solution.py:177
  9.9 2.0 %collective-permute-start = (bf16[4096,128]{1,0:T(8,128)(2,1)}, bf16[4096,128]{1,0:T(8,128)(2,1)}, u32[]{:S(2)}, u32[]{:S(2)}) collective-permute-start(bf16[4096,128]{1,0:T(8,128)(2,1)} %param.8), channel_id=1, source_target_pairs={{0,4},{4,8},{8,12},{12,16},{16,20},{20,24},{24,28},{28,0},{32,60},... | collective-permute-start | bytes 3145736 | tf_op jit(solution)/shard_map/ppermute | solution.py:24
  14.6 4.1 %gather_fusion = bf16[96,4,896]{2,1,0:T(4,128)(2,1)} fusion(bf16[512,4,896]{2,1,0:T(4,128)(2,1)} %param.11, s32[1024]{0:T(1024)S(1)} %pad_clamp_fusion.1), kind=kCustom, calls=%fused_computation | custom fusion | bytes 1376640 | tf_op jit(solution)/shard_map/jit(_take)/gather | solution.py:198
  18.7 7.6 %all-to-all-start = ((bf16[96,4,896]{2,1,0:T(4,128)(2,1)}), bf16[96,4,896]{2,1,0:T(4,128)(2,1)S(1)}, u32[]{:S(2)}, u32[]{:S(2)}) async-start(bf16[96,4,896]{2,1,0:T(4,128)(2,1)} %gather_fusion), calls=%async_computation | async-start | bytes 1376256 | tf_op jit(solution)/shard_map/all_to_all | solution.py:199
  28.1 3.6 %collective-permute-start.3 = (bf16[128,1024]{1,0:T(8,128)(2,1)S(1)}, bf16[128,1024]{1,0:T(8,128)(2,1)S(1)}, u32[]{:S(2)}, u32[]{:S(2)}) collective-permute-start(bf16[128,1024]{1,0:T(8,128)(2,1)S(1)} %constant_dynamic-slice_fusion), channel_id=1, source_target_pairs={{0,8},{4,12},{8,16},{12,20},{16,24},{20,28},{24,0},{28,4},{32,56},... | collective-permute-start | bytes 786440 | tf_op jit(solution)/shard_map/ppermute | solution.py:24
  31.7 6.6 %all-to-all-done = bf16[96,4,896]{2,1,0:T(4,128)(2,1)S(1)} async-done(((bf16[96,4,896]{2,1,0:T(4,128)(2,1)}), bf16[96,4,896]{2,1,0:T(4,128)(2,1)S(1)}, u32[]{:S(2)}, u32[]{:S(2)}) %all-to-all-start) | async-done | bytes 688160 | tf_op jit(solution)/shard_map/all_to_all | solution.py:199
  38.4 1.7 gather_fusion.1
  40.1 1.7 collective-permute-done.2
  41.8 4.2 %collective-permute-start.4 = (bf16[4096,128]{1,0:T(8,128)(2,1)}, bf16[4096,128]{1,0:T(8,128)(2,1)}, u32[]{:S(2)}, u32[]{:S(2)}) collective-permute-start(bf16[4096,128]{1,0:T(8,128)(2,1)} %collective-permute-done), channel_id=1, source_target_pairs={{0,4},{4,8},{8,12},{12,16},{16,20},{20,24},{24,28},{28,0},{32,60},... | collective-permute-start | bytes 3145736 | tf_op jit(solution)/shard_map/ppermute | solution.py:24
  45.9 4.1 %all-to-all-start.1 = ((bf16[64,4,896]{2,1,0:T(4,128)(2,1)}), bf16[64,4,896]{2,1,0:T(4,128)(2,1)S(1)}, u32[]{:S(2)}, u32[]{:S(2)}) async-start(bf16[64,4,896]{2,1,0:T(4,128)(2,1)} %gather_fusion.1), calls=%async_computation.1 | async-start | bytes 917504 | tf_op jit(solution)/shard_map/all_to_all | solution.py:215
  52.4 3.2 %collective-permute-start.12 = (bf16[2,128,1024]{2,1,0:T(8,128)(2,1)S(1)}, bf16[2,128,1024]{2,1,0:T(8,128)(2,1)}, u32[]{:S(2)}, u32[]{:S(2)}) collective-permute-start(bf16[2,128,1024]{2,1,0:T(8,128)(2,1)S(1)} %pad_maximum_fusion.refs_0_), channel_id=1, source_target_pairs={{0,192},{64,0},{128,64},{192,128},{1,193},{65,1},{129,65},{193,129... | collective-permute-start | bytes 1572872 | tf_op jit(solution)/shard_map/ppermute | solution.py:43
  55.7 2.9 %collective-permute-start.16 = (bf16[128,1024]{1,0:T(8,128)(2,1)}, bf16[128,1024]{1,0:T(8,128)(2,1)}, u32[]{:S(2)}, u32[]{:S(2)}) collective-permute-start(bf16[128,1024]{1,0:T(8,128)(2,1)} %collective-permute-done.2), channel_id=1, source_target_pairs={{0,8},{4,12},{8,16},{12,20},{16,24},{20,28},{24,0},{28,4},{32,56},... | collective-permute-start | bytes 786440 | tf_op jit(solution)/shard_map/ppermute | solution.py:24
  58.5 12.6 %all-to-all-done.1 = bf16[64,4,896]{2,1,0:T(4,128)(2,1)S(1)} async-done(((bf16[64,4,896]{2,1,0:T(4,128)(2,1)}), bf16[64,4,896]{2,1,0:T(4,128)(2,1)S(1)}, u32[]{:S(2)}, u32[]{:S(2)}) %all-to-all-start.1) | async-done | bytes 458784 | tf_op jit(solution)/shard_map/all_to_all | solution.py:215
  72.2 1.8 collective-permute-start.8
  77.4 3.2 %collective-permute-start.18 = (bf16[2,128,1024]{2,1,0:T(8,128)(2,1)S(1)}, bf16[2,128,1024]{2,1,0:T(8,128)(2,1)S(1)}, u32[]{:S(2)}, u32[]{:S(2)}) collective-permute-start(bf16[2,128,1024]{2,1,0:T(8,128)(2,1)S(1)} %pad_maximum_fusion.1.refs_5_), channel_id=1, source_target_pairs={{0,192},{64,0},{128,64},{192,128},{1,193},{65,1},{129,65},{193,129... | collective-permute-start | bytes 1572872 | tf_op jit(solution)/shard_map/ppermute | solution.py:43
  82.0 1.9 %collective-permute-start.20 = (bf16[2,128,1024]{2,1,0:T(8,128)(2,1)S(1)}, bf16[2,128,1024]{2,1,0:T(8,128)(2,1)S(1)}, u32[]{:S(2)}, u32[]{:S(2)}) collective-permute-start(bf16[2,128,1024]{2,1,0:T(8,128)(2,1)S(1)} %pad_maximum_fusion.1.refs_5_), channel_id=1, source_target_pairs={{0,64},{64,128},{128,192},{192,0},{1,65},{65,129},{129,193},{193,1... | collective-permute-start | bytes 1572872 | tf_op jit(solution)/shard_map/ppermute | solution.py:43
  87.4 1.7 slice_bitcast_fusion.5
  90.8 2.4 %collective-permute-done.5 = bf16[4096,128]{1,0:T(8,128)(2,1)S(1)} collective-permute-done((bf16[4096,128]{1,0:T(8,128)(2,1)}, bf16[4096,128]{1,0:T(8,128)(2,1)S(1)}, u32[]{:S(2)}, u32[]{:S(2)}) %collective-permute-start.5) | collective-permute-done | bytes 1048608 | tf_op jit(solution)/shard_map/ppermute | solution.py:24
  94.0 8.1 %collective-permute-start.7 = (bf16[2048,128]{1,0:T(8,128)(2,1)S(1)}, bf16[2048,128]{1,0:T(8,128)(2,1)S(1)}, u32[]{:S(2)}, u32[]{:S(2)}) collective-permute-start(bf16[2048,128]{1,0:T(8,128)(2,1)S(1)} %get-tuple-element.22), channel_id=1, source_target_pairs={{0,36},{4,40},{8,44},{12,48},{16,52},{20,56},{24,60},{28,32},{1,37... | collective-permute-start | bytes 1572872 | tf_op jit(solution)/shard_map/ppermute | solution.py:24
  102.9 3.6 %collective-permute-start.11 = (bf16[1,896,128]{2,1,0:T(8,128)(2,1)S(1)}, bf16[1,896,128]{2,1,0:T(8,128)(2,1)S(1)}, u32[]{:S(2)}, u32[]{:S(2)}) collective-permute-start(bf16[1,896,128]{2,1,0:T(8,128)(2,1)S(1)} %get-tuple-element.26), channel_id=1, source_target_pairs={{0,36},{4,40},{8,44},{12,48},{16,52},{20,56},{24,60},{28,32},{1,37... | collective-permute-start | bytes 688136 | tf_op jit(solution)/shard_map/ppermute | solution.py:24
  108.9 2.3 %collective-permute-done.11 = bf16[1,896,128]{2,1,0:T(8,128)(2,1)S(1)} collective-permute-done((bf16[1,896,128]{2,1,0:T(8,128)(2,1)S(1)}, bf16[1,896,128]{2,1,0:T(8,128)(2,1)S(1)}, u32[]{:S(2)}, u32[]{:S(2)}) %collective-permute-start.11) | collective-permute-done | bytes 229408 | tf_op jit(solution)/shard_map/ppermute | solution.py:24
  111.2 3.8 %collective-permute-start.19 = (bf16[128,1024]{1,0:T(8,128)(2,1)}, bf16[128,1024]{1,0:T(8,128)(2,1)}, u32[]{:S(2)}, u32[]{:S(2)}) collective-permute-start(bf16[128,1024]{1,0:T(8,128)(2,1)} %slice_bitcast_fusion.4), channel_id=1, source_target_pairs={{0,192},{64,0},{128,64},{192,128},{1,193},{65,1},{129,65},{193,129... | collective-permute-start | bytes 786440 | tf_op jit(solution)/shard_map/ppermute | solution.py:43
  117.8 3.6 %fusion.2.q2 = bf16[512,128]{1,0:T(8,128)(2,1)S(1)} fusion(bf16[512,4096]{1,0:T(8,128)(2,1)} %all-gather.3.cloned.1.call-done, bf16[4096,128]{1,0:T(8,128)(2,1)S(1)} %collective-permute-done.5), kind=kOutput, calls=%fused_computation.13 | convolution fusion | flops 537001984 | bytes 5373952 | tf_op jit(solution)/shard_map/dot_general | solution.py:162
  121.4 2.5 %fusion.1.q1 = bf16[512,128]{1,0:T(8,128)(2,1)S(1)} fusion(bf16[512,4096]{1,0:T(8,128)(2,1)S(1)} %copy-done.10, bf16[4096,128]{1,0:T(8,128)(2,1)} %collective-permute-done.4), kind=kOutput, calls=%fused_computation.12 | convolution fusion | flops 537001984 | bytes 5373952 | tf_op jit(solution)/shard_map/dot_general | solution.py:162
  123.9 2.5 %fusion.q0 = bf16[512,128]{1,0:T(8,128)(2,1)S(1)} fusion(bf16[512,4096]{1,0:T(8,128)(2,1)S(1)} %copy-done.10, bf16[4096,128]{1,0:T(8,128)(2,1)} %collective-permute-done), kind=kOutput, calls=%fused_computation.11 | convolution fusion | flops 537001984 | bytes 5373952 | tf_op jit(solution)/shard_map/dot_general | solution.py:162
  127.0 4.5 %shard_map.73 = bf16[512,4096]{1,0:T(8,128)(2,1)} custom-call(s32[3]{0:T(128)} %pad_add_fusion.place, bf16[2,128,1024]{2,1,0:T(8,128)(2,1)} %copy-done.5, bf16[2,128,1024]{2,1,0:T(8,128)(2,1)} %collective-permute-done.12.refs_1_, bf16[128,1024]{1,0:T(8,128)(2,1)} %collective-permute-done.13.refs_2_, bf16[128,1024]{1,0:T(8,128)(2,1)} %collective-permute-done.15.refs_3_, ...), custom_call_target="tpu_custom_call" | custom-call | flops 17999998976 | bytes 10000 | tf_op jit(solution)/shard_map/pallas_call | solution.py:71
  131.4 3.4 %fusion.3.q3 = bf16[512,128]{1,0:T(8,128)(2,1)S(1)} fusion(bf16[512,4096]{1,0:T(8,128)(2,1)} %all-gather.3.cloned.1.call-done, bf16[4096,128]{1,0:T(8,128)(2,1)S(1)} %copy-done.4), kind=kOutput, calls=%fused_computation.14 | convolution fusion | flops 537001984 | bytes 5373952 | tf_op jit(solution)/shard_map/dot_general | solution.py:162
  134.9 2.0 %copy-done = bf16[64,32,896]{2,1,0:T(8,128)(2,1)S(1)} copy-done((bf16[64,32,896]{2,1,0:T(8,128)(2,1)S(1)}, bf16[64,32,896]{2,1,0:T(8,128)(2,1)}, u32[]{:S(2)}) %copy-start) | copy-done | bytes 3670040
  136.9 11.4 %shard_map.74 = bf16[512,512]{1,0:T(8,128)(2,1)S(1)} custom-call(s32[3]{0:T(128)S(1)} %copy-done.1, bf16[512,128]{1,0:T(8,128)(2,1)S(1)} %fusion.q0, bf16[512,128]{1,0:T(8,128)(2,1)S(1)} %fusion.1.q1, bf16[512,128]{1,0:T(8,128)(2,1)S(1)} %fusion.2.q2, bf16[512,128]{1,0:T(8,128)(2,1)S(1)} %fusion.3.q3, bf16[2,896,128]{2,1,0:T(8,128)(2,1)S(1)} %collective-permute-done.1.kv0, ...), custom_call_target="tpu_custom_call" | custom-call | flops 1000000 | bytes 10000 | tf_op jit(solution)/shard_map/pallas_call | solution.py:118
  154.7 5.5 %collective-permute-done.24 = bf16[64,2048]{1,0:T(8,128)(2,1)S(1)} collective-permute-done((bf16[64,2048]{1,0:T(8,128)(2,1)S(1)}, bf16[64,2048]{1,0:T(8,128)(2,1)S(1)}, u32[]{:S(2)}, u32[]{:S(2)}) %collective-permute-start.24) | collective-permute-done | bytes 262176 | tf_op jit(solution)/shard_map/ppermute | solution.py:43
  162.4 1.7 collective-permute-start.27
  164.1 11.0 %collective-permute-done.25 = bf16[64,4096]{1,0:T(8,128)(2,1)S(1)} collective-permute-done((bf16[64,4096]{1,0:T(8,128)(2,1)S(1)}, bf16[64,4096]{1,0:T(8,128)(2,1)S(1)}, u32[]{:S(2)}, u32[]{:S(2)}) %collective-permute-start.25) | collective-permute-done | bytes 524320 | tf_op jit(solution)/shard_map/ppermute | solution.py:43
  (103 shorter events, 37.4 us)
Async XLA Ops:
  6.5 111.2 %all-gather.3.cloned.1.call-start = ((), (), s32[]{:S(2)}) async-start(), calls=%async_computation.2 | async-start | bytes 4718592 | tf_op jit(solution)/shard_map/all_gather | solution.py:178
  9.9 31.9 %collective-permute-start = (bf16[4096,128]{1,0:T(8,128)(2,1)}, bf16[4096,128]{1,0:T(8,128)(2,1)}, u32[]{:S(2)}, u32[]{:S(2)}) collective-permute-start(bf16[4096,128]{1,0:T(8,128)(2,1)} %param.8), channel_id=1, source_target_pairs={{0,4},{4,8},{8,12},{12,16},{16,20},{20,24},{24,28},{28,0},{32,60},... | collective-permute-start | bytes 3145736 | tf_op jit(solution)/shard_map/ppermute | solution.py:24
  18.7 19.7 %all-to-all-start = ((bf16[96,4,896]{2,1,0:T(4,128)(2,1)}), bf16[96,4,896]{2,1,0:T(4,128)(2,1)S(1)}, u32[]{:S(2)}, u32[]{:S(2)}) async-start(bf16[96,4,896]{2,1,0:T(4,128)(2,1)} %gather_fusion), calls=%async_computation | async-start | bytes 1376256 | tf_op jit(solution)/shard_map/all_to_all | solution.py:199
  26.3 15.5 %collective-permute-start.1 = (bf16[2,896,128]{2,1,0:T(8,128)(2,1)S(1)}, bf16[2,896,128]{2,1,0:T(8,128)(2,1)S(1)}, u32[]{:S(2)}, u32[]{:S(2)}) collective-permute-start(bf16[2,896,128]{2,1,0:T(8,128)(2,1)S(1)} %copy-done.7), channel_id=1, source_target_pairs={{0,4},{4,8},{8,12},{12,16},{16,20},{20,24},{24,28},{28,0},{32,60},... | collective-permute-start | bytes 1376264 | tf_op jit(solution)/shard_map/ppermute | solution.py:24
  27.3 14.4 %collective-permute-start.2 = (bf16[128,1024]{1,0:T(8,128)(2,1)S(1)}, bf16[128,1024]{1,0:T(8,128)(2,1)}, u32[]{:S(2)}, u32[]{:S(2)}) collective-permute-start(bf16[128,1024]{1,0:T(8,128)(2,1)S(1)} %constant_dynamic-slice_fusion), channel_id=1, source_target_pairs={{0,4},{4,8},{8,12},{12,16},{16,20},{20,24},{24,28},{28,0},{32,60},... | collective-permute-start | bytes 786440 | tf_op jit(solution)/shard_map/ppermute | solution.py:24
  28.1 13.6 %collective-permute-start.3 = (bf16[128,1024]{1,0:T(8,128)(2,1)S(1)}, bf16[128,1024]{1,0:T(8,128)(2,1)S(1)}, u32[]{:S(2)}, u32[]{:S(2)}) collective-permute-start(bf16[128,1024]{1,0:T(8,128)(2,1)S(1)} %constant_dynamic-slice_fusion), channel_id=1, source_target_pairs={{0,8},{4,12},{8,16},{12,20},{16,24},{20,28},{24,0},{28,4},{32,56},... | collective-permute-start | bytes 786440 | tf_op jit(solution)/shard_map/ppermute | solution.py:24
  41.8 32.3 %collective-permute-start.4 = (bf16[4096,128]{1,0:T(8,128)(2,1)}, bf16[4096,128]{1,0:T(8,128)(2,1)}, u32[]{:S(2)}, u32[]{:S(2)}) collective-permute-start(bf16[4096,128]{1,0:T(8,128)(2,1)} %collective-permute-done), channel_id=1, source_target_pairs={{0,4},{4,8},{8,12},{12,16},{16,20},{20,24},{24,28},{28,0},{32,60},... | collective-permute-start | bytes 3145736 | tf_op jit(solution)/shard_map/ppermute | solution.py:24
  45.9 25.2 %all-to-all-start.1 = ((bf16[64,4,896]{2,1,0:T(4,128)(2,1)}), bf16[64,4,896]{2,1,0:T(4,128)(2,1)S(1)}, u32[]{:S(2)}, u32[]{:S(2)}) async-start(bf16[64,4,896]{2,1,0:T(4,128)(2,1)} %gather_fusion.1), calls=%async_computation.1 | async-start | bytes 917504 | tf_op jit(solution)/shard_map/all_to_all | solution.py:215
  50.0 84.9 %all-gather.5.cloned.1.call-start = ((), (), s32[]{:S(2)}) async-start(), calls=%async_computation.3 | async-start | bytes 4128768 | tf_op jit(solution)/shard_map/all_gather | solution.py:246
  50.0 22.2 %collective-permute-start.17 = (bf16[128,1024]{1,0:T(8,128)(2,1)S(1)}, bf16[128,1024]{1,0:T(8,128)(2,1)}, u32[]{:S(2)}, u32[]{:S(2)}) collective-permute-start(bf16[128,1024]{1,0:T(8,128)(2,1)S(1)} %collective-permute-done.3), channel_id=1, source_target_pairs={{32,56},{36,60},{40,32},{44,36},{48,40},{52,44},{56,48},{60,52},{3... | collective-permute-start | bytes 786440 | tf_op jit(solution)/shard_map/ppermute | solution.py:24
  52.4 31.5 %collective-permute-start.12 = (bf16[2,128,1024]{2,1,0:T(8,128)(2,1)S(1)}, bf16[2,128,1024]{2,1,0:T(8,128)(2,1)}, u32[]{:S(2)}, u32[]{:S(2)}) collective-permute-start(bf16[2,128,1024]{2,1,0:T(8,128)(2,1)S(1)} %pad_maximum_fusion.refs_0_), channel_id=1, source_target_pairs={{0,192},{64,0},{128,64},{192,128},{1,193},{65,1},{129,65},{193,129... | collective-permute-start | bytes 1572872 | tf_op jit(solution)/shard_map/ppermute | solution.py:43
  55.7 20.7 %collective-permute-start.16 = (bf16[128,1024]{1,0:T(8,128)(2,1)}, bf16[128,1024]{1,0:T(8,128)(2,1)}, u32[]{:S(2)}, u32[]{:S(2)}) collective-permute-start(bf16[128,1024]{1,0:T(8,128)(2,1)} %collective-permute-done.2), channel_id=1, source_target_pairs={{0,8},{4,12},{8,16},{12,20},{16,24},{20,28},{24,0},{28,4},{32,56},... | collective-permute-start | bytes 786440 | tf_op jit(solution)/shard_map/ppermute | solution.py:24
  58.5 27.6 %collective-permute-start.14 = (bf16[2,128,1024]{2,1,0:T(8,128)(2,1)S(1)}, bf16[2,128,1024]{2,1,0:T(8,128)(2,1)}, u32[]{:S(2)}, u32[]{:S(2)}) collective-permute-start(bf16[2,128,1024]{2,1,0:T(8,128)(2,1)S(1)} %pad_maximum_fusion.refs_0_), channel_id=1, source_target_pairs={{0,64},{64,128},{128,192},{192,0},{1,65},{65,129},{129,193},{193,1... | collective-permute-start | bytes 1572872 | tf_op jit(solution)/shard_map/ppermute | solution.py:43
  72.2 9.8 %collective-permute-start.8 = (bf16[2,896,128]{2,1,0:T(8,128)(2,1)S(1)}, bf16[2,896,128]{2,1,0:T(8,128)(2,1)S(1)}, u32[]{:S(2)}, u32[]{:S(2)}) collective-permute-start(bf16[2,896,128]{2,1,0:T(8,128)(2,1)S(1)} %collective-permute-done.1.kv0), channel_id=1, source_target_pairs={{0,4},{4,8},{8,12},{12,16},{16,20},{20,24},{24,28},{28,0},{32,60},... | collective-permute-start | bytes 1376264 | tf_op jit(solution)/shard_map/ppermute | solution.py:24
  74.1 19.2 %collective-permute-start.5 = (bf16[4096,128]{1,0:T(8,128)(2,1)}, bf16[4096,128]{1,0:T(8,128)(2,1)S(1)}, u32[]{:S(2)}, u32[]{:S(2)}) collective-permute-start(bf16[4096,128]{1,0:T(8,128)(2,1)} %collective-permute-done.4), channel_id=1, source_target_pairs={{0,4},{4,8},{8,12},{12,16},{16,20},{20,24},{24,28},{28,0},{32,60},... | collective-permute-start | bytes 3145736 | tf_op jit(solution)/shard_map/ppermute | solution.py:24
  77.4 12.4 %collective-permute-start.18 = (bf16[2,128,1024]{2,1,0:T(8,128)(2,1)S(1)}, bf16[2,128,1024]{2,1,0:T(8,128)(2,1)S(1)}, u32[]{:S(2)}, u32[]{:S(2)}) collective-permute-start(bf16[2,128,1024]{2,1,0:T(8,128)(2,1)S(1)} %pad_maximum_fusion.1.refs_5_), channel_id=1, source_target_pairs={{0,192},{64,0},{128,64},{192,128},{1,193},{65,1},{129,65},{193,129... | collective-permute-start | bytes 1572872 | tf_op jit(solution)/shard_map/ppermute | solution.py:43
  82.0 20.9 %collective-permute-start.20 = (bf16[2,128,1024]{2,1,0:T(8,128)(2,1)S(1)}, bf16[2,128,1024]{2,1,0:T(8,128)(2,1)S(1)}, u32[]{:S(2)}, u32[]{:S(2)}) collective-permute-start(bf16[2,128,1024]{2,1,0:T(8,128)(2,1)S(1)} %pad_maximum_fusion.1.refs_5_), channel_id=1, source_target_pairs={{0,64},{64,128},{128,192},{192,0},{1,65},{65,129},{129,193},{193,1... | collective-permute-start | bytes 1572872 | tf_op jit(solution)/shard_map/ppermute | solution.py:43
  83.9 18.2 %collective-permute-start.9 = (bf16[2,896,128]{2,1,0:T(8,128)(2,1)S(1)}, bf16[2,896,128]{2,1,0:T(8,128)(2,1)S(1)}, u32[]{:S(2)}, u32[]{:S(2)}) collective-permute-start(bf16[2,896,128]{2,1,0:T(8,128)(2,1)S(1)} %collective-permute-done.8.kv1), channel_id=1, source_target_pairs={{0,4},{4,8},{8,12},{12,16},{16,20},{20,24},{24,28},{28,0},{32,60},... | collective-permute-start | bytes 1376264 | tf_op jit(solution)/shard_map/ppermute | solution.py:24
  86.1 40.2 %collective-permute-start.13 = (bf16[128,1024]{1,0:T(8,128)(2,1)}, bf16[128,1024]{1,0:T(8,128)(2,1)}, u32[]{:S(2)}, u32[]{:S(2)}) collective-permute-start(bf16[128,1024]{1,0:T(8,128)(2,1)} %slice_bitcast_fusion.6), channel_id=1, source_target_pairs={{0,192},{64,0},{128,64},{192,128},{1,193},{65,1},{129,65},{193,129... | collective-permute-start | bytes 786440 | tf_op jit(solution)/shard_map/ppermute | solution.py:43
  93.3 22.8 %collective-permute-start.6 = (bf16[2048,128]{1,0:T(8,128)(2,1)S(1)}, bf16[2048,128]{1,0:T(8,128)(2,1)S(1)}, u32[]{:S(2)}, u32[]{:S(2)}) collective-permute-start(bf16[2048,128]{1,0:T(8,128)(2,1)S(1)} %get-tuple-element.21), channel_id=1, source_target_pairs={{32,60},{36,32},{40,36},{44,40},{48,44},{52,48},{56,52},{60,56},{3... | collective-permute-start | bytes 1572872 | tf_op jit(solution)/shard_map/ppermute | solution.py:24
  94.0 22.4 %collective-permute-start.7 = (bf16[2048,128]{1,0:T(8,128)(2,1)S(1)}, bf16[2048,128]{1,0:T(8,128)(2,1)S(1)}, u32[]{:S(2)}, u32[]{:S(2)}) collective-permute-start(bf16[2048,128]{1,0:T(8,128)(2,1)S(1)} %get-tuple-element.22), channel_id=1, source_target_pairs={{0,36},{4,40},{8,44},{12,48},{16,52},{20,56},{24,60},{28,32},{1,37... | collective-permute-start | bytes 1572872 | tf_op jit(solution)/shard_map/ppermute | solution.py:24
  102.2 5.1 %collective-permute-start.10 = (bf16[1,896,128]{2,1,0:T(8,128)(2,1)S(1)}, bf16[1,896,128]{2,1,0:T(8,128)(2,1)S(1)}, u32[]{:S(2)}, u32[]{:S(2)}) collective-permute-start(bf16[1,896,128]{2,1,0:T(8,128)(2,1)S(1)} %get-tuple-element.25), channel_id=1, source_target_pairs={{32,60},{36,32},{40,36},{44,40},{48,44},{52,48},{56,52},{60,56},{3... | collective-permute-start | bytes 688136 | tf_op jit(solution)/shard_map/ppermute | solution.py:24
  102.9 8.3 %collective-permute-start.11 = (bf16[1,896,128]{2,1,0:T(8,128)(2,1)S(1)}, bf16[1,896,128]{2,1,0:T(8,128)(2,1)S(1)}, u32[]{:S(2)}, u32[]{:S(2)}) collective-permute-start(bf16[1,896,128]{2,1,0:T(8,128)(2,1)S(1)} %get-tuple-element.26), channel_id=1, source_target_pairs={{0,36},{4,40},{8,44},{12,48},{16,52},{20,56},{24,60},{28,32},{1,37... | collective-permute-start | bytes 688136 | tf_op jit(solution)/shard_map/ppermute | solution.py:24
  107.2 19.2 %collective-permute-start.15 = (bf16[128,1024]{1,0:T(8,128)(2,1)}, bf16[128,1024]{1,0:T(8,128)(2,1)}, u32[]{:S(2)}, u32[]{:S(2)}) collective-permute-start(bf16[128,1024]{1,0:T(8,128)(2,1)} %slice_bitcast_fusion.5), channel_id=1, source_target_pairs={{0,64},{64,128},{128,192},{192,0},{1,65},{65,129},{129,193},{193,1... | collective-permute-start | bytes 786440 | tf_op jit(solution)/shard_map/ppermute | solution.py:43
  111.2 15.2 %collective-permute-start.19 = (bf16[128,1024]{1,0:T(8,128)(2,1)}, bf16[128,1024]{1,0:T(8,128)(2,1)}, u32[]{:S(2)}, u32[]{:S(2)}) collective-permute-start(bf16[128,1024]{1,0:T(8,128)(2,1)} %slice_bitcast_fusion.4), channel_id=1, source_target_pairs={{0,192},{64,0},{128,64},{192,128},{1,193},{65,1},{129,65},{193,129... | collective-permute-start | bytes 786440 | tf_op jit(solution)/shard_map/ppermute | solution.py:43
  116.1 10.8 %collective-permute-start.21 = (bf16[128,1024]{1,0:T(8,128)(2,1)}, bf16[128,1024]{1,0:T(8,128)(2,1)}, u32[]{:S(2)}, u32[]{:S(2)}) collective-permute-start(bf16[128,1024]{1,0:T(8,128)(2,1)} %slice_bitcast_fusion.3), channel_id=1, source_target_pairs={{0,64},{64,128},{128,192},{192,0},{1,65},{65,129},{129,193},{193,1... | collective-permute-start | bytes 786440 | tf_op jit(solution)/shard_map/ppermute | solution.py:43
  149.2 2.3 %collective-permute-start.23 = (bf16[64,4096]{1,0:T(8,128)(2,1)S(1)}, bf16[64,4096]{1,0:T(8,128)(2,1)S(1)}, u32[]{:S(2)}, u32[]{:S(2)}) collective-permute-start(bf16[64,4096]{1,0:T(8,128)(2,1)S(1)} %slice.109), channel_id=1, source_target_pairs={{0,32},{32,0},{1,33},{33,1},{2,34},{34,2},{3,35},{35,3},{4,36},{36... | collective-permute-start | bytes 1572872 | tf_op jit(solution)/shard_map/ppermute | solution.py:43
  150.8 10.8 %collective-permute-start.22 = (bf16[3,64,4096]{2,1,0:T(8,128)(2,1)S(1)}, bf16[3,64,4096]{2,1,0:T(8,128)(2,1)S(1)}, u32[]{:S(2)}, u32[]{:S(2)}) collective-permute-start(bf16[3,64,4096]{2,1,0:T(8,128)(2,1)S(1)} %bitcast.53), channel_id=1, source_target_pairs={{0,32},{32,0},{1,33},{33,1},{2,34},{34,2},{3,35},{35,3},{4,36},{36... | collective-permute-start | bytes 4718600 | tf_op jit(solution)/shard_map/ppermute | solution.py:43
  151.6 8.6 %collective-permute-start.24 = (bf16[64,2048]{1,0:T(8,128)(2,1)S(1)}, bf16[64,2048]{1,0:T(8,128)(2,1)S(1)}, u32[]{:S(2)}, u32[]{:S(2)}) collective-permute-start(bf16[64,2048]{1,0:T(8,128)(2,1)S(1)} %get-tuple-element.23), channel_id=1, source_target_pairs={{0,1},{1,2},{2,3},{3,0},{4,5},{5,6},{6,7},{7,4},{8,9},{9,10},{10,1... | collective-permute-start | bytes 786440 | tf_op jit(solution)/shard_map/ppermute | solution.py:43
  152.1 9.5 %collective-permute-start.26 = (bf16[64,2048]{1,0:T(8,128)(2,1)S(1)}, bf16[64,2048]{1,0:T(8,128)(2,1)S(1)}, u32[]{:S(2)}, u32[]{:S(2)}) collective-permute-start(bf16[64,2048]{1,0:T(8,128)(2,1)S(1)} %get-tuple-element.24), channel_id=1, source_target_pairs={{0,3},{1,0},{2,1},{3,2},{4,7},{5,4},{6,5},{7,6},{8,11},{9,8},{10,9... | collective-permute-start | bytes 786440 | tf_op jit(solution)/shard_map/ppermute | solution.py:43
  162.0 13.1 %collective-permute-start.25 = (bf16[64,4096]{1,0:T(8,128)(2,1)S(1)}, bf16[64,4096]{1,0:T(8,128)(2,1)S(1)}, u32[]{:S(2)}, u32[]{:S(2)}) collective-permute-start(bf16[64,4096]{1,0:T(8,128)(2,1)S(1)} %get-tuple-element.19), channel_id=1, source_target_pairs={{0,1},{1,2},{2,3},{3,0},{4,5},{5,6},{6,7},{7,4},{8,9},{9,10},{10,1... | collective-permute-start | bytes 1572872 | tf_op jit(solution)/shard_map/ppermute | solution.py:43
  162.4 14.3 %collective-permute-start.27 = (bf16[64,4096]{1,0:T(8,128)(2,1)S(1)}, bf16[64,4096]{1,0:T(8,128)(2,1)S(1)}, u32[]{:S(2)}, u32[]{:S(2)}) collective-permute-start(bf16[64,4096]{1,0:T(8,128)(2,1)S(1)} %get-tuple-element.20), channel_id=1, source_target_pairs={{0,3},{1,0},{2,1},{3,2},{4,7},{5,4},{6,5},{7,6},{8,11},{9,8},{10,9... | collective-permute-start | bytes 1572872 | tf_op jit(solution)/shard_map/ppermute | solution.py:43
  (11 other events, 187.3 us)
Sparse Core Ops, SparseCore 0:
  10.0 35.6 all-gather.2
  72.3 32.9 all-gather.4

commit v3 on v2

--- a/solution.py
+++ b/solution.py
@@ -52,7 +52,7 @@
 
 
 OUT_COLS = D // Y
-UNPACK_FLOPS = 18_000_000_000
+UNPACK_FLOPS = 21_000_000_000
 
 
 def unpack_kernel(place, *refs):
@@ -98,19 +98,25 @@
             jnp.bfloat16
         )
         first = pl.multiple_of((core * X + block) * BLOCK, BLOCK)
-        for h, q_h in enumerate((q0, q1, q2, q3)):
-            keys = keys_values[:, 2 * h * HD : (2 * h + 1) * HD]
-            values = keys_values[:, (2 * h + 1) * HD : (2 * h + 2) * HD]
-            scores = lax.dot_general(
-                q_h[pl.ds(first, BLOCK), :],
-                keys,
-                (((1,), (1,)), ((), ())),
+        scores = jnp.concatenate(
+            [
+                lax.dot_general(
+                    q_h[pl.ds(first, BLOCK), :],
+                    keys_values[:, 2 * h * HD : (2 * h + 1) * HD],
+                    (((1,), (1,)), ((), ())),
+                    preferred_element_type=jnp.float32,
+                )
+                for h, q_h in enumerate((q0, q1, q2, q3))
+            ],
+            axis=0,
+        )
+        expo = jnp.exp(scores)
+        weights = (expo / jnp.sum(expo, axis=1, keepdims=True)).astype(jnp.bfloat16)
+        for h in range(HEADS_HERE):
+            attended[j * BLOCK : (j + 1) * BLOCK, h * HD : (h + 1) * HD] = jnp.dot(
+                weights[h * BLOCK : (h + 1) * BLOCK],
+                keys_values[:, (2 * h + 1) * HD : (2 * h + 2) * HD],
                 preferred_element_type=jnp.float32,
-            )
-            expo = jnp.exp(scores)
-            weights = (expo / jnp.sum(expo, axis=1, keepdims=True)).astype(jnp.bfloat16)
-            attended[j * BLOCK : (j + 1) * BLOCK, h * HD : (h + 1) * HD] = jnp.dot(
-                weights, values, preferred_element_type=jnp.float32
             ).astype(jnp.bfloat16)
 
 
@@ -227,17 +233,16 @@
     far_pair = jnp.stack([out_third, out_last])
     far_up = shift(far_pair, "y", -1)
     far_down = shift(far_pair, "y", 1)
+    queries.append(project_queries(rows, q_second))
     near0 = shift(near_up[0], "y", -1)
     near1 = shift(near_down[1], "y", 1)
-    queries.append(project_queries(rows, q_second))
     q_third, kv_third = q_hops[2], kv_hops[2]
-    q_last = last_hop(q_weight, q_third)
+    q_last = last_hop(q_weight, tie(q_third, *queries))
     kv_last = last_hop(kv_weight, kv_third)
     far0 = shift(far_up[0], "y", -1)
     far1 = shift(far_down[1], "y", 1)
     queries.append(project_queries(rows, q_third))
     place_then = tie(place, q_last, kv_last, *queries)
-    queries.append(project_queries(rows, q_last))
     kv_pieces = [kv_first, kv_second, kv_third, kv_last]
     wo = unpack(
         place_then,
@@ -247,6 +252,7 @@
         C, X, X, NEIGH, Z * own_tokens, ENC
     )
 
+    queries.append(project_queries(rows, tie(q_last, neighbours)))
     attended = attend(tie(place, wo), queries, kv_pieces, neighbours)
     return project_and_reduce(attended, wo)
 

time: 185 us -> 182 us (0.984)
  waiting for transfers between devices: 47.6 us -> 58.7 us
  starting transfers between devices: 63.9 us -> 58.4 us
  local copies, waits for them, and re-layouts: 17.1 us -> 13.3 us
  Pallas kernels: 15.9 us -> 12.9 us
  other arithmetic: 11.5 us -> 9.57 us
    ppermute x14, waiting for transfers between devices: 21.1 us -> 31.9 us  [shift(): lax.ppermute(value, axis, [(i, (i + by) % size) for i in range(size)])]
    all_to_all x1, waiting for transfers between devices: 12.6 us -> 4.72 us  [body(): lax.all_to_all(wanted, 'z', split_axis=0, concat_axis=0, tiled=True)]
    ppermute x14, waiting for transfers between devices: 7.19 us -> 14.5 us  [move(): lax.ppermute(value, ('c', 'z'), [(c * Z + z, d * Z + w % Z) for c, z, d,...]
    ppermute x14, starting transfers between devices: 31.6 us -> 25.6 us  [move(): lax.ppermute(value, ('c', 'z'), [(c * Z + z, d * Z + w % Z) for c, z, d,...]
    all_to_all x1, starting transfers between devices: 4.06 us -> 7.86 us  [body(): lax.all_to_all(wanted, 'z', split_axis=0, concat_axis=0, tiled=True)]
    ppermute x14, starting transfers between devices: 20.6 us -> 17.3 us  [shift(): lax.ppermute(value, axis, [(i, (i + by) % size) for i in range(size)])]
    pallas_call x1, Pallas kernels: 11.4 us -> 8.48 us  [attend(): pl.pallas_call(attend_kernel, in_specs=[IN_SMEM] + [IN_VMEM] * (2 * HEADS...]
    unnamed x24 -> x30, local copies, waits for them, and re-layouts: 3.84 us -> 1.68 us
  transfers between devices with their start and end apart: 32 -> 32, of which waited for: 13 -> 14; matrix products, arithmetic and copies ran while one was open for 19% -> 15% of each run, Pallas kernels for 2% -> 2%
where the time goes in v3:
time: 182 us; the launch traced here: 181 us
  waiting for transfers between devices  58.7 us (32%)
  starting transfers between devices  58.4 us (32%)
  matrix products  14 us (8%)
  between operations  13.9 us (8%)
  local copies, waits for them, and re-layouts  13.3 us (7%)
  Pallas kernels  12.9 us (7%)
  other arithmetic  9.57 us (5%)
    ppermute x14, waiting for transfers between devices, shift(): lax.ppermute(value, axis, [(i, (i + by) % size) for i in range(size)])  31.9 us
    ppermute x14, starting transfers between devices, move(): lax.ppermute(value, ('c', 'z'), [(c * Z + z, d * Z + w % Z) for c, z, d,...  25.6 us
    ppermute x14, starting transfers between devices, shift(): lax.ppermute(value, axis, [(i, (i + by) % size) for i in range(size)])  17.3 us
    ppermute x14, waiting for transfers between devices, move(): lax.ppermute(value, ('c', 'z'), [(c * Z + z, d * Z + w % Z) for c, z, d,...  14.5 us
    dot_general x4, matrix products, project_queries(): wide = jnp.dot(rows, weight, preferred_element_type=jnp.float32)  11.3 us
    pallas_call x1, Pallas kernels, attend(): pl.pallas_call(attend_kernel, in_specs=[IN_SMEM] + [IN_VMEM] * (2 * HEADS...  8.48 us
    all_to_all x1, starting transfers between devices, body(): lax.all_to_all(wanted, 'z', split_axis=0, concat_axis=0, tiled=True)  7.86 us
    all_to_all x1, waiting for transfers between devices, body(): lax.all_to_all(outgoing, ('y', 'c'), split_axis=0, concat_axis=0, tiled=T...  7.58 us
  transfers between devices with their start and end apart: 32, of which 14 were waited for; matrix products, arithmetic and copies ran while one was open for 15% of the time, Pallas kernels for 2%

profile of v3, /device:TPU:6, one launch (start us, length us, event | category | flops | bytes accessed | tf_op | source)
XLA Modules:
  0.0 180.8 jit_solution(363700296253811057)
XLA Ops:
  7.9 2.0 %fusion.5 = bf16[64,4096]{1,0:T(8,128)(2,1)} fusion(bf16[64,4096]{1,0:T(8,128)(2,1)} %param.7, f32[64]{0:T(128)S(1)} %add_rsqrt_fusion), kind=kLoop, calls=%fused_computation.16 | loop fusion | flops 786432 | bytes 1048832 | tf_op jit(solution)/shard_map/convert_element_type | solution.py:183
  9.9 2.0 %collective-permute-start = (bf16[4096,128]{1,0:T(8,128)(2,1)}, bf16[4096,128]{1,0:T(8,128)(2,1)}, u32[]{:S(2)}, u32[]{:S(2)}) collective-permute-start(bf16[4096,128]{1,0:T(8,128)(2,1)} %param.8), channel_id=1, source_target_pairs={{0,4},{4,8},{8,12},{12,16},{16,20},{20,24},{24,28},{28,0},{32,60},... | collective-permute-start | bytes 3145736 | tf_op jit(solution)/shard_map/ppermute | solution.py:24
  14.6 4.1 %gather_fusion = bf16[96,4,896]{2,1,0:T(4,128)(2,1)} fusion(bf16[512,4,896]{2,1,0:T(4,128)(2,1)} %param.11, s32[1024]{0:T(1024)S(1)} %pad_clamp_fusion.1), kind=kCustom, calls=%fused_computation | custom fusion | bytes 1376640 | tf_op jit(solution)/shard_map/jit(_take)/gather | solution.py:204
  18.8 7.6 %all-to-all-start = ((bf16[96,4,896]{2,1,0:T(4,128)(2,1)}), bf16[96,4,896]{2,1,0:T(4,128)(2,1)S(1)}, u32[]{:S(2)}, u32[]{:S(2)}) async-start(bf16[96,4,896]{2,1,0:T(4,128)(2,1)} %gather_fusion), calls=%async_computation | async-start | bytes 1376256 | tf_op jit(solution)/shard_map/all_to_all | solution.py:205
  27.2 3.6 %collective-permute-start.3 = (bf16[128,1024]{1,0:T(8,128)(2,1)S(1)}, bf16[128,1024]{1,0:T(8,128)(2,1)}, u32[]{:S(2)}, u32[]{:S(2)}) collective-permute-start(bf16[128,1024]{1,0:T(8,128)(2,1)S(1)} %constant_dynamic-slice_fusion), channel_id=1, source_target_pairs={{0,8},{4,12},{8,16},{12,20},{16,24},{20,28},{24,0},{28,4},{32,56},... | collective-permute-start | bytes 786440 | tf_op jit(solution)/shard_map/ppermute | solution.py:24
  30.8 7.6 %all-to-all-done = bf16[96,4,896]{2,1,0:T(4,128)(2,1)S(1)} async-done(((bf16[96,4,896]{2,1,0:T(4,128)(2,1)}), bf16[96,4,896]{2,1,0:T(4,128)(2,1)S(1)}, u32[]{:S(2)}, u32[]{:S(2)}) %all-to-all-start) | async-done | bytes 688160 | tf_op jit(solution)/shard_map/all_to_all | solution.py:205
  38.4 1.7 gather_fusion.1
  41.7 7.9 %all-to-all-start.1 = ((bf16[64,4,896]{2,1,0:T(4,128)(2,1)}), bf16[64,4,896]{2,1,0:T(4,128)(2,1)S(1)}, u32[]{:S(2)}, u32[]{:S(2)}) async-start(bf16[64,4,896]{2,1,0:T(4,128)(2,1)} %gather_fusion.1), calls=%async_computation.1 | async-start | bytes 917504 | tf_op jit(solution)/shard_map/all_to_all | solution.py:221
  52.1 3.2 %collective-permute-start.12 = (bf16[2,128,1024]{2,1,0:T(8,128)(2,1)S(1)}, bf16[2,128,1024]{2,1,0:T(8,128)(2,1)}, u32[]{:S(2)}, u32[]{:S(2)}) collective-permute-start(bf16[2,128,1024]{2,1,0:T(8,128)(2,1)S(1)} %pad_maximum_fusion.refs_0_), channel_id=1, source_target_pairs={{0,192},{64,0},{128,64},{192,128},{1,193},{65,1},{129,65},{193,129... | collective-permute-start | bytes 1572872 | tf_op jit(solution)/shard_map/ppermute | solution.py:43
  55.3 2.9 %collective-permute-start.16 = (bf16[128,1024]{1,0:T(8,128)(2,1)}, bf16[128,1024]{1,0:T(8,128)(2,1)}, u32[]{:S(2)}, u32[]{:S(2)}) collective-permute-start(bf16[128,1024]{1,0:T(8,128)(2,1)} %copy-done.10), channel_id=1, source_target_pairs={{0,8},{4,12},{8,16},{12,20},{16,24},{20,28},{24,0},{28,4},{32,56},... | collective-permute-start | bytes 786440 | tf_op jit(solution)/shard_map/ppermute | solution.py:24
  59.7 4.7 %all-to-all-done.1 = bf16[64,4,896]{2,1,0:T(4,128)(2,1)S(1)} async-done(((bf16[64,4,896]{2,1,0:T(4,128)(2,1)}), bf16[64,4,896]{2,1,0:T(4,128)(2,1)S(1)}, u32[]{:S(2)}, u32[]{:S(2)}) %all-to-all-start.1) | async-done | bytes 458784 | tf_op jit(solution)/shard_map/all_to_all | solution.py:221
  65.5 5.2 %collective-permute-start.4 = (bf16[4096,128]{1,0:T(8,128)(2,1)}, bf16[4096,128]{1,0:T(8,128)(2,1)}, u32[]{:S(2)}, u32[]{:S(2)}) collective-permute-start(bf16[4096,128]{1,0:T(8,128)(2,1)} %collective-permute-done), channel_id=1, source_target_pairs={{0,4},{4,8},{8,12},{12,16},{16,20},{20,24},{24,28},{28,0},{32,60},... | collective-permute-start | bytes 3145736 | tf_op jit(solution)/shard_map/ppermute | solution.py:24
  71.8 3.2 %collective-permute-start.18 = (bf16[2,128,1024]{2,1,0:T(8,128)(2,1)S(1)}, bf16[2,128,1024]{2,1,0:T(8,128)(2,1)S(1)}, u32[]{:S(2)}, u32[]{:S(2)}) collective-permute-start(bf16[2,128,1024]{2,1,0:T(8,128)(2,1)S(1)} %pad_maximum_fusion.1.refs_5_), channel_id=1, source_target_pairs={{0,192},{64,0},{128,64},{192,128},{1,193},{65,1},{129,65},{193,129... | collective-permute-start | bytes 1572872 | tf_op jit(solution)/shard_map/ppermute | solution.py:43
  76.9 3.1 %collective-permute-start.13 = (bf16[128,1024]{1,0:T(8,128)(2,1)S(1)}, bf16[128,1024]{1,0:T(8,128)(2,1)}, u32[]{:S(2)}, u32[]{:S(2)}) collective-permute-start(bf16[128,1024]{1,0:T(8,128)(2,1)S(1)} %slice_bitcast_fusion.6), channel_id=1, source_target_pairs={{0,192},{64,0},{128,64},{192,128},{1,193},{65,1},{129,65},{193,129... | collective-permute-start | bytes 786440 | tf_op jit(solution)/shard_map/ppermute | solution.py:43
  79.9 1.7 slice_bitcast_fusion.5
  81.6 5.0 %collective-permute-done.18.refs_6_ = bf16[2,128,1024]{2,1,0:T(8,128)(2,1)S(1)} collective-permute-done((bf16[2,128,1024]{2,1,0:T(8,128)(2,1)S(1)}, bf16[2,128,1024]{2,1,0:T(8,128)(2,1)S(1)}, u32[]{:S(2)}, u32[]{:S(2)}) %collective-permute-start.18) | collective-permute-done | bytes 524320 | tf_op jit(solution)/shard_map/ppermute | solution.py:43
  88.6 2.6 %collective-permute-done.20.refs_9_ = bf16[2,128,1024]{2,1,0:T(8,128)(2,1)S(1)} collective-permute-done((bf16[2,128,1024]{2,1,0:T(8,128)(2,1)S(1)}, bf16[2,128,1024]{2,1,0:T(8,128)(2,1)S(1)}, u32[]{:S(2)}, u32[]{:S(2)}) %collective-permute-start.20) | collective-permute-done | bytes 524320 | tf_op jit(solution)/shard_map/ppermute | solution.py:43
  93.6 3.9 %fusion.1.q1 = bf16[512,128]{1,0:T(8,128)(2,1)S(1)} fusion(bf16[512,4096]{1,0:T(8,128)(2,1)} %all-gather.3.cloned.1.call-done, bf16[4096,128]{1,0:T(8,128)(2,1)} %collective-permute-done.4), kind=kOutput, calls=%fused_computation.12 | convolution fusion | flops 537001984 | bytes 5373952 | tf_op jit(solution)/shard_map/dot_general | solution.py:168
  97.5 2.5 %fusion.q0 = bf16[512,128]{1,0:T(8,128)(2,1)S(1)} fusion(bf16[512,4096]{1,0:T(8,128)(2,1)S(1)} %copy-done.13, bf16[4096,128]{1,0:T(8,128)(2,1)} %collective-permute-done), kind=kOutput, calls=%fused_computation.11 | convolution fusion | flops 537001984 | bytes 5373952 | tf_op jit(solution)/shard_map/dot_general | solution.py:168
  100.1 7.5 %collective-permute-done.5 = bf16[4096,128]{1,0:T(8,128)(2,1)S(1)} collective-permute-done((bf16[4096,128]{1,0:T(8,128)(2,1)}, bf16[4096,128]{1,0:T(8,128)(2,1)S(1)}, u32[]{:S(2)}, u32[]{:S(2)}) %collective-permute-start.5) | collective-permute-done | bytes 1048608 | tf_op jit(solution)/shard_map/ppermute | solution.py:24
  107.6 2.0 %collective-permute-start.11 = (bf16[1,896,128]{2,1,0:T(8,128)(2,1)S(1)}, bf16[1,896,128]{2,1,0:T(8,128)(2,1)S(1)}, u32[]{:S(2)}, u32[]{:S(2)}) collective-permute-start(bf16[1,896,128]{2,1,0:T(8,128)(2,1)S(1)} %get-tuple-element.30), channel_id=1, source_target_pairs={{0,36},{4,40},{8,44},{12,48},{16,52},{20,56},{24,60},{28,32},{1,37... | collective-permute-start | bytes 688136 | tf_op jit(solution)/shard_map/ppermute | solution.py:24
  110.4 2.7 %collective-permute-done.11 = bf16[1,896,128]{2,1,0:T(8,128)(2,1)S(1)} collective-permute-done((bf16[1,896,128]{2,1,0:T(8,128)(2,1)S(1)}, bf16[1,896,128]{2,1,0:T(8,128)(2,1)S(1)}, u32[]{:S(2)}, u32[]{:S(2)}) %collective-permute-start.11) | collective-permute-done | bytes 229408 | tf_op jit(solution)/shard_map/ppermute | solution.py:24
  113.1 3.8 %collective-permute-start.7 = (bf16[2048,128]{1,0:T(8,128)(2,1)S(1)}, bf16[2048,128]{1,0:T(8,128)(2,1)S(1)}, u32[]{:S(2)}, u32[]{:S(2)}) collective-permute-start(bf16[2048,128]{1,0:T(8,128)(2,1)S(1)} %get-tuple-element.26), channel_id=1, source_target_pairs={{0,36},{4,40},{8,44},{12,48},{16,52},{20,56},{24,60},{28,32},{1,37... | collective-permute-start | bytes 1572872 | tf_op jit(solution)/shard_map/ppermute | solution.py:24
  119.3 1.7 collective-permute-start.21
  121.0 2.6 %collective-permute-done.7 = bf16[2048,128]{1,0:T(8,128)(2,1)S(1)} collective-permute-done((bf16[2048,128]{1,0:T(8,128)(2,1)S(1)}, bf16[2048,128]{1,0:T(8,128)(2,1)S(1)}, u32[]{:S(2)}, u32[]{:S(2)}) %collective-permute-start.7) | collective-permute-done | bytes 524320 | tf_op jit(solution)/shard_map/ppermute | solution.py:24
  123.9 4.8 %collective-permute-done.21.refs_8_ = bf16[128,1024]{1,0:T(8,128)(2,1)} collective-permute-done((bf16[128,1024]{1,0:T(8,128)(2,1)S(1)}, bf16[128,1024]{1,0:T(8,128)(2,1)}, u32[]{:S(2)}, u32[]{:S(2)}) %collective-permute-start.21) | collective-permute-done | bytes 262176 | tf_op jit(solution)/shard_map/ppermute | solution.py:43
  128.7 4.5 %shard_map.73 = bf16[512,4096]{1,0:T(8,128)(2,1)} custom-call(s32[3]{0:T(128)} %pad_add_fusion.place, bf16[2,128,1024]{2,1,0:T(8,128)(2,1)} %copy-done.4, bf16[2,128,1024]{2,1,0:T(8,128)(2,1)} %collective-permute-done.12.refs_1_, bf16[128,1024]{1,0:T(8,128)(2,1)} %collective-permute-done.13.refs_2_, bf16[128,1024]{1,0:T(8,128)(2,1)} %collective-permute-done.15.refs_3_, ...), custom_call_target="tpu_custom_call" | custom-call | flops 20999999488 | bytes 10000 | tf_op jit(solution)/shard_map/pallas_call | solution.py:71
  133.2 3.6 %fusion.3.q3 = bf16[512,128]{1,0:T(8,128)(2,1)S(1)} fusion(bf16[512,4096]{1,0:T(8,128)(2,1)} %all-gather.3.cloned.1.call-done, bf16[4096,128]{1,0:T(8,128)(2,1)S(1)} %maximum_select_fusion), kind=kOutput, calls=%fused_computation.14 | convolution fusion | flops 537001984 | bytes 5373952 | tf_op jit(solution)/shard_map/dot_general | solution.py:168
  136.8 8.5 %shard_map.74 = bf16[512,512]{1,0:T(8,128)(2,1)S(1)} custom-call(s32[3]{0:T(128)S(1)} %copy-done.1, bf16[512,128]{1,0:T(8,128)(2,1)S(1)} %fusion.q0, bf16[512,128]{1,0:T(8,128)(2,1)S(1)} %fusion.1.q1, bf16[512,128]{1,0:T(8,128)(2,1)S(1)} %fusion.2.q2, bf16[512,128]{1,0:T(8,128)(2,1)S(1)} %fusion.3.q3, bf16[2,896,128]{2,1,0:T(8,128)(2,1)S(1)} %collective-permute-done.1.kv0, ...), custom_call_target="tpu_custom_call" | custom-call | flops 1000000 | bytes 10000 | tf_op jit(solution)/shard_map/pallas_call | solution.py:124
  151.3 5.3 %collective-permute-done.24 = bf16[64,2048]{1,0:T(8,128)(2,1)S(1)} collective-permute-done((bf16[64,2048]{1,0:T(8,128)(2,1)S(1)}, bf16[64,2048]{1,0:T(8,128)(2,1)S(1)}, u32[]{:S(2)}, u32[]{:S(2)}) %collective-permute-start.24) | collective-permute-done | bytes 262176 | tf_op jit(solution)/shard_map/ppermute | solution.py:43
  158.8 1.9 %collective-permute-start.27 = (bf16[64,4096]{1,0:T(8,128)(2,1)S(1)}, bf16[64,4096]{1,0:T(8,128)(2,1)S(1)}, u32[]{:S(2)}, u32[]{:S(2)}) collective-permute-start(bf16[64,4096]{1,0:T(8,128)(2,1)S(1)} %get-tuple-element.24), channel_id=1, source_target_pairs={{0,3},{1,0},{2,1},{3,2},{4,7},{5,4},{6,5},{7,6},{8,11},{9,8},{10,9... | collective-permute-start | bytes 1572872 | tf_op jit(solution)/shard_map/ppermute | solution.py:43
  160.7 11.0 %collective-permute-done.25 = bf16[64,4096]{1,0:T(8,128)(2,1)S(1)} collective-permute-done((bf16[64,4096]{1,0:T(8,128)(2,1)S(1)}, bf16[64,4096]{1,0:T(8,128)(2,1)S(1)}, u32[]{:S(2)}, u32[]{:S(2)}) %collective-permute-start.25) | collective-permute-done | bytes 524320 | tf_op jit(solution)/shard_map/ppermute | solution.py:43
  (109 shorter events, 32.6 us)
Async XLA Ops:
  6.5 87.0 %all-gather.3.cloned.1.call-start = ((), (), s32[]{:S(2)}) async-start(), calls=%async_computation.2 | async-start | bytes 4718592 | tf_op jit(solution)/shard_map/all_gather | solution.py:184
  9.9 31.8 %collective-permute-start = (bf16[4096,128]{1,0:T(8,128)(2,1)}, bf16[4096,128]{1,0:T(8,128)(2,1)}, u32[]{:S(2)}, u32[]{:S(2)}) collective-permute-start(bf16[4096,128]{1,0:T(8,128)(2,1)} %param.8), channel_id=1, source_target_pairs={{0,4},{4,8},{8,12},{12,16},{16,20},{20,24},{24,28},{28,0},{32,60},... | collective-permute-start | bytes 3145736 | tf_op jit(solution)/shard_map/ppermute | solution.py:24
  18.8 19.7 %all-to-all-start = ((bf16[96,4,896]{2,1,0:T(4,128)(2,1)}), bf16[96,4,896]{2,1,0:T(4,128)(2,1)S(1)}, u32[]{:S(2)}, u32[]{:S(2)}) async-start(bf16[96,4,896]{2,1,0:T(4,128)(2,1)} %gather_fusion), calls=%async_computation | async-start | bytes 1376256 | tf_op jit(solution)/shard_map/all_to_all | solution.py:205
  26.3 15.4 %collective-permute-start.1 = (bf16[2,896,128]{2,1,0:T(8,128)(2,1)S(1)}, bf16[2,896,128]{2,1,0:T(8,128)(2,1)S(1)}, u32[]{:S(2)}, u32[]{:S(2)}) collective-permute-start(bf16[2,896,128]{2,1,0:T(8,128)(2,1)S(1)} %copy-done.6), channel_id=1, source_target_pairs={{0,4},{4,8},{8,12},{12,16},{16,20},{20,24},{24,28},{28,0},{32,60},... | collective-permute-start | bytes 1376264 | tf_op jit(solution)/shard_map/ppermute | solution.py:24
  26.5 15.3 %collective-permute-start.2 = (bf16[128,1024]{1,0:T(8,128)(2,1)S(1)}, bf16[128,1024]{1,0:T(8,128)(2,1)S(1)}, u32[]{:S(2)}, u32[]{:S(2)}) collective-permute-start(bf16[128,1024]{1,0:T(8,128)(2,1)S(1)} %constant_dynamic-slice_fusion), channel_id=1, source_target_pairs={{0,4},{4,8},{8,12},{12,16},{16,20},{20,24},{24,28},{28,0},{32,60},... | collective-permute-start | bytes 786440 | tf_op jit(solution)/shard_map/ppermute | solution.py:24
  27.2 14.5 %collective-permute-start.3 = (bf16[128,1024]{1,0:T(8,128)(2,1)S(1)}, bf16[128,1024]{1,0:T(8,128)(2,1)}, u32[]{:S(2)}, u32[]{:S(2)}) collective-permute-start(bf16[128,1024]{1,0:T(8,128)(2,1)S(1)} %constant_dynamic-slice_fusion), channel_id=1, source_target_pairs={{0,8},{4,12},{8,16},{12,20},{16,24},{20,28},{24,0},{28,4},{32,56},... | collective-permute-start | bytes 786440 | tf_op jit(solution)/shard_map/ppermute | solution.py:24
  41.7 22.7 %all-to-all-start.1 = ((bf16[64,4,896]{2,1,0:T(4,128)(2,1)}), bf16[64,4,896]{2,1,0:T(4,128)(2,1)S(1)}, u32[]{:S(2)}, u32[]{:S(2)}) async-start(bf16[64,4,896]{2,1,0:T(4,128)(2,1)} %gather_fusion.1), calls=%async_computation.1 | async-start | bytes 917504 | tf_op jit(solution)/shard_map/all_to_all | solution.py:221
  49.6 83.6 %all-gather.5.cloned.1.call-start = ((), (), s32[]{:S(2)}) async-start(), calls=%async_computation.3 | async-start | bytes 4128768 | tf_op jit(solution)/shard_map/all_gather | solution.py:251
  49.6 15.8 %collective-permute-start.17 = (bf16[128,1024]{1,0:T(8,128)(2,1)}, bf16[128,1024]{1,0:T(8,128)(2,1)}, u32[]{:S(2)}, u32[]{:S(2)}) collective-permute-start(bf16[128,1024]{1,0:T(8,128)(2,1)} %collective-permute-done.3), channel_id=1, source_target_pairs={{32,56},{36,60},{40,32},{44,36},{48,40},{52,44},{56,48},{60,52},{3... | collective-permute-start | bytes 786440 | tf_op jit(solution)/shard_map/ppermute | solution.py:24
  52.1 23.5 %collective-permute-start.12 = (bf16[2,128,1024]{2,1,0:T(8,128)(2,1)S(1)}, bf16[2,128,1024]{2,1,0:T(8,128)(2,1)}, u32[]{:S(2)}, u32[]{:S(2)}) collective-permute-start(bf16[2,128,1024]{2,1,0:T(8,128)(2,1)S(1)} %pad_maximum_fusion.refs_0_), channel_id=1, source_target_pairs={{0,192},{64,0},{128,64},{192,128},{1,193},{65,1},{129,65},{193,129... | collective-permute-start | bytes 1572872 | tf_op jit(solution)/shard_map/ppermute | solution.py:43
  55.3 15.4 %collective-permute-start.16 = (bf16[128,1024]{1,0:T(8,128)(2,1)}, bf16[128,1024]{1,0:T(8,128)(2,1)}, u32[]{:S(2)}, u32[]{:S(2)}) collective-permute-start(bf16[128,1024]{1,0:T(8,128)(2,1)} %copy-done.10), channel_id=1, source_target_pairs={{0,8},{4,12},{8,16},{12,20},{16,24},{20,28},{24,0},{28,4},{32,56},... | collective-permute-start | bytes 786440 | tf_op jit(solution)/shard_map/ppermute | solution.py:24
  58.2 18.6 %collective-permute-start.14 = (bf16[2,128,1024]{2,1,0:T(8,128)(2,1)S(1)}, bf16[2,128,1024]{2,1,0:T(8,128)(2,1)}, u32[]{:S(2)}, u32[]{:S(2)}) collective-permute-start(bf16[2,128,1024]{2,1,0:T(8,128)(2,1)S(1)} %pad_maximum_fusion.refs_0_), channel_id=1, source_target_pairs={{0,64},{64,128},{128,192},{192,0},{1,65},{65,129},{129,193},{193,1... | collective-permute-start | bytes 1572872 | tf_op jit(solution)/shard_map/ppermute | solution.py:43
  58.2 17.4 %collective-permute-start.8 = (bf16[2,896,128]{2,1,0:T(8,128)(2,1)S(1)}, bf16[2,896,128]{2,1,0:T(8,128)(2,1)S(1)}, u32[]{:S(2)}, u32[]{:S(2)}) collective-permute-start(bf16[2,896,128]{2,1,0:T(8,128)(2,1)S(1)} %collective-permute-done.1.kv0), channel_id=1, source_target_pairs={{0,4},{4,8},{8,12},{12,16},{16,20},{20,24},{24,28},{28,0},{32,60},... | collective-permute-start | bytes 1376264 | tf_op jit(solution)/shard_map/ppermute | solution.py:24
  65.5 25.8 %collective-permute-start.4 = (bf16[4096,128]{1,0:T(8,128)(2,1)}, bf16[4096,128]{1,0:T(8,128)(2,1)}, u32[]{:S(2)}, u32[]{:S(2)}) collective-permute-start(bf16[4096,128]{1,0:T(8,128)(2,1)} %collective-permute-done), channel_id=1, source_target_pairs={{0,4},{4,8},{8,12},{12,16},{16,20},{20,24},{24,28},{28,0},{32,60},... | collective-permute-start | bytes 3145736 | tf_op jit(solution)/shard_map/ppermute | solution.py:24
  71.8 14.8 %collective-permute-start.18 = (bf16[2,128,1024]{2,1,0:T(8,128)(2,1)S(1)}, bf16[2,128,1024]{2,1,0:T(8,128)(2,1)S(1)}, u32[]{:S(2)}, u32[]{:S(2)}) collective-permute-start(bf16[2,128,1024]{2,1,0:T(8,128)(2,1)S(1)} %pad_maximum_fusion.1.refs_5_), channel_id=1, source_target_pairs={{0,192},{64,0},{128,64},{192,128},{1,193},{65,1},{129,65},{193,129... | collective-permute-start | bytes 1572872 | tf_op jit(solution)/shard_map/ppermute | solution.py:43
  75.6 15.7 %collective-permute-start.20 = (bf16[2,128,1024]{2,1,0:T(8,128)(2,1)S(1)}, bf16[2,128,1024]{2,1,0:T(8,128)(2,1)S(1)}, u32[]{:S(2)}, u32[]{:S(2)}) collective-permute-start(bf16[2,128,1024]{2,1,0:T(8,128)(2,1)S(1)} %pad_maximum_fusion.1.refs_5_), channel_id=1, source_target_pairs={{0,64},{64,128},{128,192},{192,0},{1,65},{65,129},{129,193},{193,1... | collective-permute-start | bytes 1572872 | tf_op jit(solution)/shard_map/ppermute | solution.py:43
  75.6 16.6 %collective-permute-start.9 = (bf16[2,896,128]{2,1,0:T(8,128)(2,1)S(1)}, bf16[2,896,128]{2,1,0:T(8,128)(2,1)S(1)}, u32[]{:S(2)}, u32[]{:S(2)}) collective-permute-start(bf16[2,896,128]{2,1,0:T(8,128)(2,1)S(1)} %collective-permute-done.8.kv1), channel_id=1, source_target_pairs={{0,4},{4,8},{8,12},{12,16},{16,20},{20,24},{24,28},{28,0},{32,60},... | collective-permute-start | bytes 1376264 | tf_op jit(solution)/shard_map/ppermute | solution.py:24
  76.9 47.0 %collective-permute-start.13 = (bf16[128,1024]{1,0:T(8,128)(2,1)S(1)}, bf16[128,1024]{1,0:T(8,128)(2,1)}, u32[]{:S(2)}, u32[]{:S(2)}) collective-permute-start(bf16[128,1024]{1,0:T(8,128)(2,1)S(1)} %slice_bitcast_fusion.6), channel_id=1, source_target_pairs={{0,192},{64,0},{128,64},{192,128},{1,193},{65,1},{129,65},{193,129... | collective-permute-start | bytes 786440 | tf_op jit(solution)/shard_map/ppermute | solution.py:43
  86.6 37.3 %collective-permute-start.15 = (bf16[128,1024]{1,0:T(8,128)(2,1)}, bf16[128,1024]{1,0:T(8,128)(2,1)}, u32[]{:S(2)}, u32[]{:S(2)}) collective-permute-start(bf16[128,1024]{1,0:T(8,128)(2,1)} %slice_bitcast_fusion.5), channel_id=1, source_target_pairs={{0,64},{64,128},{128,192},{192,0},{1,65},{65,129},{129,193},{193,1... | collective-permute-start | bytes 786440 | tf_op jit(solution)/shard_map/ppermute | solution.py:43
  91.2 32.7 %collective-permute-start.19 = (bf16[128,1024]{1,0:T(8,128)(2,1)}, bf16[128,1024]{1,0:T(8,128)(2,1)}, u32[]{:S(2)}, u32[]{:S(2)}) collective-permute-start(bf16[128,1024]{1,0:T(8,128)(2,1)} %slice_bitcast_fusion.4), channel_id=1, source_target_pairs={{0,192},{64,0},{128,64},{192,128},{1,193},{65,1},{129,65},{193,129... | collective-permute-start | bytes 786440 | tf_op jit(solution)/shard_map/ppermute | solution.py:43
  91.3 16.3 %collective-permute-start.5 = (bf16[4096,128]{1,0:T(8,128)(2,1)}, bf16[4096,128]{1,0:T(8,128)(2,1)S(1)}, u32[]{:S(2)}, u32[]{:S(2)}) collective-permute-start(bf16[4096,128]{1,0:T(8,128)(2,1)} %collective-permute-done.4), channel_id=1, source_target_pairs={{0,4},{4,8},{8,12},{12,16},{16,20},{20,24},{24,28},{28,0},{32,60},... | collective-permute-start | bytes 3145736 | tf_op jit(solution)/shard_map/ppermute | solution.py:24
  92.2 17.5 %collective-permute-start.10 = (bf16[1,896,128]{2,1,0:T(8,128)(2,1)S(1)}, bf16[1,896,128]{2,1,0:T(8,128)(2,1)}, u32[]{:S(2)}, u32[]{:S(2)}) collective-permute-start(bf16[1,896,128]{2,1,0:T(8,128)(2,1)S(1)} %get-tuple-element.29), channel_id=1, source_target_pairs={{32,60},{36,32},{40,36},{44,40},{48,44},{52,48},{56,52},{60,56},{3... | collective-permute-start | bytes 688136 | tf_op jit(solution)/shard_map/ppermute | solution.py:24
  107.6 5.5 %collective-permute-start.11 = (bf16[1,896,128]{2,1,0:T(8,128)(2,1)S(1)}, bf16[1,896,128]{2,1,0:T(8,128)(2,1)S(1)}, u32[]{:S(2)}, u32[]{:S(2)}) collective-permute-start(bf16[1,896,128]{2,1,0:T(8,128)(2,1)S(1)} %get-tuple-element.30), channel_id=1, source_target_pairs={{0,36},{4,40},{8,44},{12,48},{16,52},{20,56},{24,60},{28,32},{1,37... | collective-permute-start | bytes 688136 | tf_op jit(solution)/shard_map/ppermute | solution.py:24
  109.7 9.5 %collective-permute-start.6 = (bf16[2048,128]{1,0:T(8,128)(2,1)S(1)}, bf16[2048,128]{1,0:T(8,128)(2,1)S(1)}, u32[]{:S(2)}, u32[]{:S(2)}) collective-permute-start(bf16[2048,128]{1,0:T(8,128)(2,1)S(1)} %get-tuple-element.25), channel_id=1, source_target_pairs={{32,60},{36,32},{40,36},{44,40},{48,44},{52,48},{56,52},{60,56},{3... | collective-permute-start | bytes 1572872 | tf_op jit(solution)/shard_map/ppermute | solution.py:24
  113.1 10.5 %collective-permute-start.7 = (bf16[2048,128]{1,0:T(8,128)(2,1)S(1)}, bf16[2048,128]{1,0:T(8,128)(2,1)S(1)}, u32[]{:S(2)}, u32[]{:S(2)}) collective-permute-start(bf16[2048,128]{1,0:T(8,128)(2,1)S(1)} %get-tuple-element.26), channel_id=1, source_target_pairs={{0,36},{4,40},{8,44},{12,48},{16,52},{20,56},{24,60},{28,32},{1,37... | collective-permute-start | bytes 1572872 | tf_op jit(solution)/shard_map/ppermute | solution.py:24
  119.3 9.4 %collective-permute-start.21 = (bf16[128,1024]{1,0:T(8,128)(2,1)S(1)}, bf16[128,1024]{1,0:T(8,128)(2,1)}, u32[]{:S(2)}, u32[]{:S(2)}) collective-permute-start(bf16[128,1024]{1,0:T(8,128)(2,1)S(1)} %copy-done.9), channel_id=1, source_target_pairs={{0,64},{64,128},{128,192},{192,0},{1,65},{65,129},{129,193},{193,1... | collective-permute-start | bytes 786440 | tf_op jit(solution)/shard_map/ppermute | solution.py:43
  146.0 2.0 %collective-permute-start.23 = (bf16[64,4096]{1,0:T(8,128)(2,1)S(1)}, bf16[64,4096]{1,0:T(8,128)(2,1)S(1)}, u32[]{:S(2)}, u32[]{:S(2)}) collective-permute-start(bf16[64,4096]{1,0:T(8,128)(2,1)S(1)} %slice.107), channel_id=1, source_target_pairs={{0,32},{32,0},{1,33},{33,1},{2,34},{34,2},{3,35},{35,3},{4,36},{36... | collective-permute-start | bytes 1572872 | tf_op jit(solution)/shard_map/ppermute | solution.py:43
  147.1 11.1 %collective-permute-start.22 = (bf16[3,64,4096]{2,1,0:T(8,128)(2,1)S(1)}, bf16[3,64,4096]{2,1,0:T(8,128)(2,1)S(1)}, u32[]{:S(2)}, u32[]{:S(2)}) collective-permute-start(bf16[3,64,4096]{2,1,0:T(8,128)(2,1)S(1)} %bitcast.53), channel_id=1, source_target_pairs={{0,32},{32,0},{1,33},{33,1},{2,34},{34,2},{3,35},{35,3},{4,36},{36... | collective-permute-start | bytes 4718600 | tf_op jit(solution)/shard_map/ppermute | solution.py:43
  148.2 8.4 %collective-permute-start.24 = (bf16[64,2048]{1,0:T(8,128)(2,1)S(1)}, bf16[64,2048]{1,0:T(8,128)(2,1)S(1)}, u32[]{:S(2)}, u32[]{:S(2)}) collective-permute-start(bf16[64,2048]{1,0:T(8,128)(2,1)S(1)} %get-tuple-element.27), channel_id=1, source_target_pairs={{0,1},{1,2},{2,3},{3,0},{4,5},{5,6},{6,7},{7,4},{8,9},{9,10},{10,1... | collective-permute-start | bytes 786440 | tf_op jit(solution)/shard_map/ppermute | solution.py:43
  148.8 9.4 %collective-permute-start.26 = (bf16[64,2048]{1,0:T(8,128)(2,1)S(1)}, bf16[64,2048]{1,0:T(8,128)(2,1)S(1)}, u32[]{:S(2)}, u32[]{:S(2)}) collective-permute-start(bf16[64,2048]{1,0:T(8,128)(2,1)S(1)} %get-tuple-element.28), channel_id=1, source_target_pairs={{0,3},{1,0},{2,1},{3,2},{4,7},{5,4},{6,5},{7,6},{8,11},{9,8},{10,9... | collective-permute-start | bytes 786440 | tf_op jit(solution)/shard_map/ppermute | solution.py:43
  158.6 13.1 %collective-permute-start.25 = (bf16[64,4096]{1,0:T(8,128)(2,1)S(1)}, bf16[64,4096]{1,0:T(8,128)(2,1)S(1)}, u32[]{:S(2)}, u32[]{:S(2)}) collective-permute-start(bf16[64,4096]{1,0:T(8,128)(2,1)S(1)} %get-tuple-element.23), channel_id=1, source_target_pairs={{0,1},{1,2},{2,3},{3,0},{4,5},{5,6},{6,7},{7,4},{8,9},{9,10},{10,1... | collective-permute-start | bytes 1572872 | tf_op jit(solution)/shard_map/ppermute | solution.py:43
  158.8 14.2 %collective-permute-start.27 = (bf16[64,4096]{1,0:T(8,128)(2,1)S(1)}, bf16[64,4096]{1,0:T(8,128)(2,1)S(1)}, u32[]{:S(2)}, u32[]{:S(2)}) collective-permute-start(bf16[64,4096]{1,0:T(8,128)(2,1)S(1)} %get-tuple-element.24), channel_id=1, source_target_pairs={{0,3},{1,0},{2,1},{3,2},{4,7},{5,4},{6,5},{7,6},{8,11},{9,8},{10,9... | collective-permute-start | bytes 1572872 | tf_op jit(solution)/shard_map/ppermute | solution.py:43
  (14 other events, 180.9 us)
Sparse Core Ops, SparseCore 0:
  10.1 35.6 all-gather.2
  65.6 31.8 all-gather.4

commit v4 on v3

--- a/solution.py
+++ b/solution.py
@@ -52,7 +52,7 @@
 
 
 OUT_COLS = D // Y
-UNPACK_FLOPS = 21_000_000_000
+UNPACK_FLOPS = 24_000_000_000
 
 
 def unpack_kernel(place, *refs):
@@ -73,6 +73,7 @@
         in_specs=[IN_SMEM] + [IN_VMEM] * len(pieces),
         out_specs=IN_VMEM,
         out_shape=jax.ShapeDtypeStruct((HEADS_HERE * HD, D), jnp.bfloat16),
+        compiler_params=pltpu.CompilerParams(vmem_limit_bytes=12 << 20),
         cost_estimate=pl.CostEstimate(
             flops=UNPACK_FLOPS, bytes_accessed=10_000, transcendentals=0
         ),
@@ -127,7 +128,7 @@
         out_specs=IN_VMEM,
         out_shape=jax.ShapeDtypeStruct((GROUP * BLOCK, HEADS_HERE * HD), jnp.bfloat16),
         scratch_shapes=[pltpu.VMEM((ENC, 2 * HEADS_HERE * HD), jnp.bfloat16)],
-        compiler_params=pltpu.CompilerParams(vmem_limit_bytes=24 << 20),
+        compiler_params=pltpu.CompilerParams(vmem_limit_bytes=12 << 20),
         cost_estimate=pl.CostEstimate(
             flops=1_000_000, bytes_accessed=10_000, transcendentals=0
         ),

time: 182 us -> 182 us (level)
  waiting for transfers between devices: 58.7 us -> 49.8 us
  starting transfers between devices: 58.4 us -> 63.8 us
  local copies, waits for them, and re-layouts: 13.3 us -> 17.3 us
  matrix products: 14 us -> 17 us
  Pallas kernels: 12.9 us -> 10 us
    ppermute x14, starting transfers between devices: 25.6 us -> 32.1 us  [move(): lax.ppermute(value, ('c', 'z'), [(c * Z + z, d * Z + w % Z) for c, z, d,...]
    ppermute x14, waiting for transfers between devices: 31.9 us -> 28.1 us  [shift(): lax.ppermute(value, axis, [(i, (i + by) % size) for i in range(size)])]
    dot_general x4, matrix products: 11.3 us -> 14.3 us  [project_queries(): wide = jnp.dot(rows, weight, preferred_element_type=jnp.float32)]
    pallas_call x1, Pallas kernels: 4.47 us -> 1.58 us  [unpack(): pl.pallas_call(unpack_kernel, in_specs=[IN_SMEM] + [IN_VMEM] * len(pieces...]
    ppermute x14, waiting for transfers between devices: 14.5 us -> 12.3 us  [move(): lax.ppermute(value, ('c', 'z'), [(c * Z + z, d * Z + w % Z) for c, z, d,...]
    unnamed x30, local copies, waits for them, and re-layouts: 1.68 us -> 3.73 us
    all_to_all x1, waiting for transfers between devices: 4.72 us -> 2.82 us  [body(): lax.all_to_all(wanted, 'z', split_axis=0, concat_axis=0, tiled=True)]
  transfers between devices with their start and end apart: 32 -> 32, of which waited for: 14 -> 15; matrix products, arithmetic and copies ran while one was open for 15% -> 18% of each run, Pallas kernels for 2% -> 1%
where the time goes in v4:
time: 182 us
  starting transfers between devices  63.8 us (35%)
  waiting for transfers between devices  49.8 us (27%)
  local copies, waits for them, and re-layouts  17.3 us (10%)
  matrix products  17 us (9%)
  between operations  13.8 us (8%)
  Pallas kernels  10 us (5%)
  other arithmetic  9.86 us (5%)
    ppermute x14, starting transfers between devices, move(): lax.ppermute(value, ('c', 'z'), [(c * Z + z, d * Z + w % Z) for c, z, d,...  32.1 us
    ppermute x14, waiting for transfers between devices, shift(): lax.ppermute(value, axis, [(i, (i + by) % size) for i in range(size)])  28.1 us
    ppermute x14, starting transfers between devices, shift(): lax.ppermute(value, axis, [(i, (i + by) % size) for i in range(size)])  16.3 us
    dot_general x4, matrix products, project_queries(): wide = jnp.dot(rows, weight, preferred_element_type=jnp.float32)  14.3 us
    ppermute x14, waiting for transfers between devices, move(): lax.ppermute(value, ('c', 'z'), [(c * Z + z, d * Z + w % Z) for c, z, d,...  12.3 us
    pallas_call x1, Pallas kernels, attend(): pl.pallas_call(attend_kernel, in_specs=[IN_SMEM] + [IN_VMEM] * (2 * HEADS...  8.43 us
    all_to_all x1, starting transfers between devices, body(): lax.all_to_all(wanted, 'z', split_axis=0, concat_axis=0, tiled=True)  7.76 us
    all_to_all x1, starting transfers between devices, body(): lax.all_to_all(outgoing, ('y', 'c'), split_axis=0, concat_axis=0, tiled=T...  7.57 us
  transfers between devices with their start and end apart: 32, of which 15 were waited for; matrix products, arithmetic and copies ran while one was open for 18% of the time, Pallas kernels for 1%

profile of v4, /device:TPU:6, one launch (start us, length us, event | category | flops | bytes accessed | tf_op | source)
XLA Modules:
  0.0 181.6 jit_solution(8566274666054332344)
XLA Ops:
  7.9 2.0 %fusion.5 = bf16[64,4096]{1,0:T(8,128)(2,1)} fusion(bf16[64,4096]{1,0:T(8,128)(2,1)} %param.7, f32[64]{0:T(128)S(1)} %add_rsqrt_fusion), kind=kLoop, calls=%fused_computation.16 | loop fusion | flops 786432 | bytes 1048832 | tf_op jit(solution)/shard_map/convert_element_type | solution.py:184
  9.9 2.0 %collective-permute-start = (bf16[4096,128]{1,0:T(8,128)(2,1)}, bf16[4096,128]{1,0:T(8,128)(2,1)}, u32[]{:S(2)}, u32[]{:S(2)}) collective-permute-start(bf16[4096,128]{1,0:T(8,128)(2,1)} %param.8), channel_id=1, source_target_pairs={{0,4},{4,8},{8,12},{12,16},{16,20},{20,24},{24,28},{28,0},{32,60},... | collective-permute-start | bytes 3145736 | tf_op jit(solution)/shard_map/ppermute | solution.py:24
  14.6 4.2 %gather_fusion = bf16[96,4,896]{2,1,0:T(4,128)(2,1)} fusion(bf16[512,4,896]{2,1,0:T(4,128)(2,1)} %param.11, s32[1024]{0:T(1024)S(1)} %pad_clamp_fusion.1), kind=kCustom, calls=%fused_computation | custom fusion | bytes 1376640 | tf_op jit(solution)/shard_map/jit(_take)/gather | solution.py:205
  18.7 7.6 %all-to-all-start = ((bf16[96,4,896]{2,1,0:T(4,128)(2,1)}), bf16[96,4,896]{2,1,0:T(4,128)(2,1)S(1)}, u32[]{:S(2)}, u32[]{:S(2)}) async-start(bf16[96,4,896]{2,1,0:T(4,128)(2,1)} %gather_fusion), calls=%async_computation | async-start | bytes 1376256 | tf_op jit(solution)/shard_map/all_to_all | solution.py:206
  28.2 3.5 %collective-permute-start.3 = (bf16[128,1024]{1,0:T(8,128)(2,1)S(1)}, bf16[128,1024]{1,0:T(8,128)(2,1)S(1)}, u32[]{:S(2)}, u32[]{:S(2)}) collective-permute-start(bf16[128,1024]{1,0:T(8,128)(2,1)S(1)} %constant_dynamic-slice_fusion), channel_id=1, source_target_pairs={{0,8},{4,12},{8,16},{12,20},{16,24},{20,28},{24,0},{28,4},{32,56},... | collective-permute-start | bytes 786440 | tf_op jit(solution)/shard_map/ppermute | solution.py:24
  31.8 6.6 %all-to-all-done = bf16[96,4,896]{2,1,0:T(4,128)(2,1)S(1)} async-done(((bf16[96,4,896]{2,1,0:T(4,128)(2,1)}), bf16[96,4,896]{2,1,0:T(4,128)(2,1)S(1)}, u32[]{:S(2)}, u32[]{:S(2)}) %all-to-all-start) | async-done | bytes 688160 | tf_op jit(solution)/shard_map/all_to_all | solution.py:206
  38.4 1.7 gather_fusion.1
  41.7 7.8 %all-to-all-start.1 = ((bf16[64,4,896]{2,1,0:T(4,128)(2,1)}), bf16[64,4,896]{2,1,0:T(4,128)(2,1)S(1)}, u32[]{:S(2)}, u32[]{:S(2)}) async-start(bf16[64,4,896]{2,1,0:T(4,128)(2,1)} %gather_fusion.1), calls=%async_computation.1 | async-start | bytes 917504 | tf_op jit(solution)/shard_map/all_to_all | solution.py:222
  50.3 3.2 %collective-permute-start.12 = (bf16[2,128,1024]{2,1,0:T(8,128)(2,1)S(1)}, bf16[2,128,1024]{2,1,0:T(8,128)(2,1)S(1)}, u32[]{:S(2)}, u32[]{:S(2)}) collective-permute-start(bf16[2,128,1024]{2,1,0:T(8,128)(2,1)S(1)} %pad_maximum_fusion.refs_0_), channel_id=1, source_target_pairs={{0,192},{64,0},{128,64},{192,128},{1,193},{65,1},{129,65},{193,129... | collective-permute-start | bytes 1572872 | tf_op jit(solution)/shard_map/ppermute | solution.py:43
  53.5 2.9 %collective-permute-start.16 = (bf16[128,1024]{1,0:T(8,128)(2,1)S(1)}, bf16[128,1024]{1,0:T(8,128)(2,1)}, u32[]{:S(2)}, u32[]{:S(2)}) collective-permute-start(bf16[128,1024]{1,0:T(8,128)(2,1)S(1)} %collective-permute-done.2), channel_id=1, source_target_pairs={{0,8},{4,12},{8,16},{12,20},{16,24},{20,28},{24,0},{28,4},{32,56},... | collective-permute-start | bytes 786440 | tf_op jit(solution)/shard_map/ppermute | solution.py:24
  57.8 2.7 %collective-permute-start.4 = (bf16[4096,128]{1,0:T(8,128)(2,1)}, bf16[4096,128]{1,0:T(8,128)(2,1)}, u32[]{:S(2)}, u32[]{:S(2)}) collective-permute-start(bf16[4096,128]{1,0:T(8,128)(2,1)} %collective-permute-done), channel_id=1, source_target_pairs={{0,4},{4,8},{8,12},{12,16},{16,20},{20,24},{24,28},{28,0},{32,60},... | collective-permute-start | bytes 3145736 | tf_op jit(solution)/shard_map/ppermute | solution.py:24
  61.5 2.8 %all-to-all-done.1 = bf16[64,4,896]{2,1,0:T(4,128)(2,1)S(1)} async-done(((bf16[64,4,896]{2,1,0:T(4,128)(2,1)}), bf16[64,4,896]{2,1,0:T(4,128)(2,1)S(1)}, u32[]{:S(2)}, u32[]{:S(2)}) %all-to-all-start.1) | async-done | bytes 458784 | tf_op jit(solution)/shard_map/all_to_all | solution.py:222
  65.4 2.7 %collective-permute-done.16 = bf16[128,1024]{1,0:T(8,128)(2,1)} collective-permute-done((bf16[128,1024]{1,0:T(8,128)(2,1)S(1)}, bf16[128,1024]{1,0:T(8,128)(2,1)}, u32[]{:S(2)}, u32[]{:S(2)}) %collective-permute-start.16) | collective-permute-done | bytes 262176 | tf_op jit(solution)/shard_map/ppermute | solution.py:24
  69.1 2.0 %collective-permute-start.18 = (bf16[2,128,1024]{2,1,0:T(8,128)(2,1)S(1)}, bf16[2,128,1024]{2,1,0:T(8,128)(2,1)S(1)}, u32[]{:S(2)}, u32[]{:S(2)}) collective-permute-start(bf16[2,128,1024]{2,1,0:T(8,128)(2,1)S(1)} %pad_maximum_fusion.1.refs_5_), channel_id=1, source_target_pairs={{0,192},{64,0},{128,64},{192,128},{1,193},{65,1},{129,65},{193,129... | collective-permute-start | bytes 1572872 | tf_op jit(solution)/shard_map/ppermute | solution.py:43
  75.9 3.0 %collective-permute-start.13 = (bf16[128,1024]{1,0:T(8,128)(2,1)}, bf16[128,1024]{1,0:T(8,128)(2,1)}, u32[]{:S(2)}, u32[]{:S(2)}) collective-permute-start(bf16[128,1024]{1,0:T(8,128)(2,1)} %slice_bitcast_fusion.6), channel_id=1, source_target_pairs={{0,192},{64,0},{128,64},{192,128},{1,193},{65,1},{129,65},{193,129... | collective-permute-start | bytes 786440 | tf_op jit(solution)/shard_map/ppermute | solution.py:43
  78.8 1.7 slice_bitcast_fusion.5
  81.3 2.9 %collective-permute-done.20.refs_9_ = bf16[2,128,1024]{2,1,0:T(8,128)(2,1)S(1)} collective-permute-done((bf16[2,128,1024]{2,1,0:T(8,128)(2,1)S(1)}, bf16[2,128,1024]{2,1,0:T(8,128)(2,1)S(1)}, u32[]{:S(2)}, u32[]{:S(2)}) %collective-permute-start.20) | collective-permute-done | bytes 524320 | tf_op jit(solution)/shard_map/ppermute | solution.py:43
  85.9 4.7 %collective-permute-start.5 = (bf16[4096,128]{1,0:T(8,128)(2,1)}, bf16[4096,128]{1,0:T(8,128)(2,1)}, u32[]{:S(2)}, u32[]{:S(2)}) collective-permute-start(bf16[4096,128]{1,0:T(8,128)(2,1)} %collective-permute-done.4), channel_id=1, source_target_pairs={{0,4},{4,8},{8,12},{12,16},{16,20},{20,24},{24,28},{28,0},{32,60},... | collective-permute-start | bytes 3145736 | tf_op jit(solution)/shard_map/ppermute | solution.py:24
  92.8 4.0 %fusion.1.q1 = bf16[512,128]{1,0:T(8,128)(2,1)S(1)} fusion(bf16[512,4096]{1,0:T(8,128)(2,1)} %all-gather.3.cloned.1.call-done, bf16[4096,128]{1,0:T(8,128)(2,1)} %collective-permute-done.4), kind=kOutput, calls=%fused_computation.12 | convolution fusion | flops 537001984 | bytes 5373952 | tf_op jit(solution)/shard_map/dot_general | solution.py:169
  96.8 3.2 %fusion.q0 = bf16[512,128]{1,0:T(8,128)(2,1)} fusion(bf16[512,4096]{1,0:T(8,128)(2,1)S(1)} %copy-done.13, bf16[4096,128]{1,0:T(8,128)(2,1)} %collective-permute-done), kind=kOutput, calls=%fused_computation.11 | convolution fusion | flops 537001984 | bytes 5373952 | tf_op jit(solution)/shard_map/dot_general | solution.py:169
  100.0 3.3 %collective-permute-done.5 = bf16[4096,128]{1,0:T(8,128)(2,1)} collective-permute-done((bf16[4096,128]{1,0:T(8,128)(2,1)}, bf16[4096,128]{1,0:T(8,128)(2,1)}, u32[]{:S(2)}, u32[]{:S(2)}) %collective-permute-start.5) | collective-permute-done | bytes 1048608 | tf_op jit(solution)/shard_map/ppermute | solution.py:24
  103.3 5.8 %collective-permute-start.11 = (bf16[1,896,128]{2,1,0:T(8,128)(2,1)S(1)}, bf16[1,896,128]{2,1,0:T(8,128)(2,1)S(1)}, u32[]{:S(2)}, u32[]{:S(2)}) collective-permute-start(bf16[1,896,128]{2,1,0:T(8,128)(2,1)S(1)} %get-tuple-element.30), channel_id=1, source_target_pairs={{0,36},{4,40},{8,44},{12,48},{16,52},{20,56},{24,60},{28,32},{1,37... | collective-permute-start | bytes 688136 | tf_op jit(solution)/shard_map/ppermute | solution.py:24
  112.6 3.8 %collective-permute-start.7 = (bf16[2048,128]{1,0:T(8,128)(2,1)S(1)}, bf16[2048,128]{1,0:T(8,128)(2,1)S(1)}, u32[]{:S(2)}, u32[]{:S(2)}) collective-permute-start(bf16[2048,128]{1,0:T(8,128)(2,1)S(1)} %get-tuple-element.26), channel_id=1, source_target_pairs={{0,36},{4,40},{8,44},{12,48},{16,52},{20,56},{24,60},{28,32},{1,37... | collective-permute-start | bytes 1572872 | tf_op jit(solution)/shard_map/ppermute | solution.py:24
  117.5 3.2 %fusion.2.q2 = bf16[512,128]{1,0:T(8,128)(2,1)} fusion(bf16[512,4096]{1,0:T(8,128)(2,1)S(1)} %copy-done.13, bf16[4096,128]{1,0:T(8,128)(2,1)} %collective-permute-done.5), kind=kOutput, calls=%fused_computation.13 | convolution fusion | flops 537001984 | bytes 5373952 | tf_op jit(solution)/shard_map/dot_general | solution.py:169
  120.7 2.4 %collective-permute-done.7 = bf16[2048,128]{1,0:T(8,128)(2,1)S(1)} collective-permute-done((bf16[2048,128]{1,0:T(8,128)(2,1)S(1)}, bf16[2048,128]{1,0:T(8,128)(2,1)S(1)}, u32[]{:S(2)}, u32[]{:S(2)}) %collective-permute-start.7) | collective-permute-done | bytes 524320 | tf_op jit(solution)/shard_map/ppermute | solution.py:24
  124.3 5.6 %collective-permute-done.21.refs_8_ = bf16[128,1024]{1,0:T(8,128)(2,1)S(1)} collective-permute-done((bf16[128,1024]{1,0:T(8,128)(2,1)S(1)}, bf16[128,1024]{1,0:T(8,128)(2,1)S(1)}, u32[]{:S(2)}, u32[]{:S(2)}) %collective-permute-start.21) | collective-permute-done | bytes 262176 | tf_op jit(solution)/shard_map/ppermute | solution.py:43
  131.6 2.1 %copy-done = bf16[512,4096]{1,0:T(8,128)(2,1)} copy-done((bf16[512,4096]{1,0:T(8,128)(2,1)}, bf16[512,4096]{1,0:T(8,128)(2,1)S(1)}, u32[]{:S(2)}) %copy-start) | copy-done | bytes 4194328
  133.6 3.9 %fusion.3.q3 = bf16[512,128]{1,0:T(8,128)(2,1)S(1)} fusion(bf16[512,4096]{1,0:T(8,128)(2,1)} %all-gather.3.cloned.1.call-done, bf16[4096,128]{1,0:T(8,128)(2,1)} %maximum_select_fusion), kind=kOutput, calls=%fused_computation.14 | convolution fusion | flops 537001984 | bytes 5373952 | tf_op jit(solution)/shard_map/dot_general | solution.py:169
  137.6 8.4 %shard_map.74 = bf16[512,512]{1,0:T(8,128)(2,1)S(1)} custom-call(s32[3]{0:T(128)S(1)} %pad_add_fusion.place, bf16[512,128]{1,0:T(8,128)(2,1)S(1)} %copy-done.7, bf16[512,128]{1,0:T(8,128)(2,1)S(1)} %fusion.1.q1, bf16[512,128]{1,0:T(8,128)(2,1)S(1)} %copy-done.8, bf16[512,128]{1,0:T(8,128)(2,1)S(1)} %fusion.3.q3, ...), custom_call_target="tpu_custom_call" | custom-call | flops 1000000 | bytes 10000 | tf_op jit(solution)/shard_map/pallas_call | solution.py:125
  152.1 5.3 %collective-permute-done.24 = bf16[64,2048]{1,0:T(8,128)(2,1)S(1)} collective-permute-done((bf16[64,2048]{1,0:T(8,128)(2,1)S(1)}, bf16[64,2048]{1,0:T(8,128)(2,1)S(1)}, u32[]{:S(2)}, u32[]{:S(2)}) %collective-permute-start.24) | collective-permute-done | bytes 262176 | tf_op jit(solution)/shard_map/ppermute | solution.py:43
  159.5 1.9 %collective-permute-start.27 = (bf16[64,4096]{1,0:T(8,128)(2,1)S(1)}, bf16[64,4096]{1,0:T(8,128)(2,1)S(1)}, u32[]{:S(2)}, u32[]{:S(2)}) collective-permute-start(bf16[64,4096]{1,0:T(8,128)(2,1)S(1)} %get-tuple-element.24), channel_id=1, source_target_pairs={{0,3},{1,0},{2,1},{3,2},{4,7},{5,4},{6,5},{7,6},{8,11},{9,8},{10,9... | collective-permute-start | bytes 1572872 | tf_op jit(solution)/shard_map/ppermute | solution.py:43
  161.4 11.0 %collective-permute-done.25 = bf16[64,4096]{1,0:T(8,128)(2,1)S(1)} collective-permute-done((bf16[64,4096]{1,0:T(8,128)(2,1)S(1)}, bf16[64,4096]{1,0:T(8,128)(2,1)S(1)}, u32[]{:S(2)}, u32[]{:S(2)}) %collective-permute-start.25) | collective-permute-done | bytes 524320 | tf_op jit(solution)/shard_map/ppermute | solution.py:43
  (109 shorter events, 40.0 us)
Async XLA Ops:
  6.5 86.2 %all-gather.3.cloned.1.call-start = ((), (), s32[]{:S(2)}) async-start(), calls=%async_computation.2 | async-start | bytes 4718592 | tf_op jit(solution)/shard_map/all_gather | solution.py:185
  9.9 31.8 %collective-permute-start = (bf16[4096,128]{1,0:T(8,128)(2,1)}, bf16[4096,128]{1,0:T(8,128)(2,1)}, u32[]{:S(2)}, u32[]{:S(2)}) collective-permute-start(bf16[4096,128]{1,0:T(8,128)(2,1)} %param.8), channel_id=1, source_target_pairs={{0,4},{4,8},{8,12},{12,16},{16,20},{20,24},{24,28},{28,0},{32,60},... | collective-permute-start | bytes 3145736 | tf_op jit(solution)/shard_map/ppermute | solution.py:24
  18.7 19.7 %all-to-all-start = ((bf16[96,4,896]{2,1,0:T(4,128)(2,1)}), bf16[96,4,896]{2,1,0:T(4,128)(2,1)S(1)}, u32[]{:S(2)}, u32[]{:S(2)}) async-start(bf16[96,4,896]{2,1,0:T(4,128)(2,1)} %gather_fusion), calls=%async_computation | async-start | bytes 1376256 | tf_op jit(solution)/shard_map/all_to_all | solution.py:206
  26.3 15.4 %collective-permute-start.1 = (bf16[2,896,128]{2,1,0:T(8,128)(2,1)S(1)}, bf16[2,896,128]{2,1,0:T(8,128)(2,1)S(1)}, u32[]{:S(2)}, u32[]{:S(2)}) collective-permute-start(bf16[2,896,128]{2,1,0:T(8,128)(2,1)S(1)} %copy-done.10), channel_id=1, source_target_pairs={{0,4},{4,8},{8,12},{12,16},{16,20},{20,24},{24,28},{28,0},{32,60},... | collective-permute-start | bytes 1376264 | tf_op jit(solution)/shard_map/ppermute | solution.py:24
  27.4 14.3 %collective-permute-start.2 = (bf16[128,1024]{1,0:T(8,128)(2,1)S(1)}, bf16[128,1024]{1,0:T(8,128)(2,1)S(1)}, u32[]{:S(2)}, u32[]{:S(2)}) collective-permute-start(bf16[128,1024]{1,0:T(8,128)(2,1)S(1)} %constant_dynamic-slice_fusion), channel_id=1, source_target_pairs={{0,4},{4,8},{8,12},{12,16},{16,20},{20,24},{24,28},{28,0},{32,60},... | collective-permute-start | bytes 786440 | tf_op jit(solution)/shard_map/ppermute | solution.py:24
  28.2 13.5 %collective-permute-start.3 = (bf16[128,1024]{1,0:T(8,128)(2,1)S(1)}, bf16[128,1024]{1,0:T(8,128)(2,1)S(1)}, u32[]{:S(2)}, u32[]{:S(2)}) collective-permute-start(bf16[128,1024]{1,0:T(8,128)(2,1)S(1)} %constant_dynamic-slice_fusion), channel_id=1, source_target_pairs={{0,8},{4,12},{8,16},{12,20},{16,24},{20,28},{24,0},{28,4},{32,56},... | collective-permute-start | bytes 786440 | tf_op jit(solution)/shard_map/ppermute | solution.py:24
  41.7 22.6 %all-to-all-start.1 = ((bf16[64,4,896]{2,1,0:T(4,128)(2,1)}), bf16[64,4,896]{2,1,0:T(4,128)(2,1)S(1)}, u32[]{:S(2)}, u32[]{:S(2)}) async-start(bf16[64,4,896]{2,1,0:T(4,128)(2,1)} %gather_fusion.1), calls=%async_computation.1 | async-start | bytes 917504 | tf_op jit(solution)/shard_map/all_to_all | solution.py:222
  49.5 84.2 %all-gather.5.cloned.1.call-start = ((), (), s32[]{:S(2)}) async-start(), calls=%async_computation.3 | async-start | bytes 4128768 | tf_op jit(solution)/shard_map/all_gather | solution.py:252
  49.5 8.3 %collective-permute-start.17 = (bf16[128,1024]{1,0:T(8,128)(2,1)S(1)}, bf16[128,1024]{1,0:T(8,128)(2,1)S(1)}, u32[]{:S(2)}, u32[]{:S(2)}) collective-permute-start(bf16[128,1024]{1,0:T(8,128)(2,1)S(1)} %collective-permute-done.3), channel_id=1, source_target_pairs={{32,56},{36,60},{40,32},{44,36},{48,40},{52,44},{56,48},{60,52},{3... | collective-permute-start | bytes 786440 | tf_op jit(solution)/shard_map/ppermute | solution.py:24
  50.3 23.4 %collective-permute-start.12 = (bf16[2,128,1024]{2,1,0:T(8,128)(2,1)S(1)}, bf16[2,128,1024]{2,1,0:T(8,128)(2,1)S(1)}, u32[]{:S(2)}, u32[]{:S(2)}) collective-permute-start(bf16[2,128,1024]{2,1,0:T(8,128)(2,1)S(1)} %pad_maximum_fusion.refs_0_), channel_id=1, source_target_pairs={{0,192},{64,0},{128,64},{192,128},{1,193},{65,1},{129,65},{193,129... | collective-permute-start | bytes 1572872 | tf_op jit(solution)/shard_map/ppermute | solution.py:43
  53.5 14.6 %collective-permute-start.16 = (bf16[128,1024]{1,0:T(8,128)(2,1)S(1)}, bf16[128,1024]{1,0:T(8,128)(2,1)}, u32[]{:S(2)}, u32[]{:S(2)}) collective-permute-start(bf16[128,1024]{1,0:T(8,128)(2,1)S(1)} %collective-permute-done.2), channel_id=1, source_target_pairs={{0,8},{4,12},{8,16},{12,20},{16,24},{20,28},{24,0},{28,4},{32,56},... | collective-permute-start | bytes 786440 | tf_op jit(solution)/shard_map/ppermute | solution.py:24
  56.4 19.5 %collective-permute-start.14 = (bf16[2,128,1024]{2,1,0:T(8,128)(2,1)S(1)}, bf16[2,128,1024]{2,1,0:T(8,128)(2,1)}, u32[]{:S(2)}, u32[]{:S(2)}) collective-permute-start(bf16[2,128,1024]{2,1,0:T(8,128)(2,1)S(1)} %pad_maximum_fusion.refs_0_), channel_id=1, source_target_pairs={{0,64},{64,128},{128,192},{192,0},{1,65},{65,129},{129,193},{193,1... | collective-permute-start | bytes 1572872 | tf_op jit(solution)/shard_map/ppermute | solution.py:43
  56.4 15.6 %collective-permute-start.8 = (bf16[2,896,128]{2,1,0:T(8,128)(2,1)S(1)}, bf16[2,896,128]{2,1,0:T(8,128)(2,1)S(1)}, u32[]{:S(2)}, u32[]{:S(2)}) collective-permute-start(bf16[2,896,128]{2,1,0:T(8,128)(2,1)S(1)} %collective-permute-done.1.kv0), channel_id=1, source_target_pairs={{0,4},{4,8},{8,12},{12,16},{16,20},{20,24},{24,28},{28,0},{32,60},... | collective-permute-start | bytes 1376264 | tf_op jit(solution)/shard_map/ppermute | solution.py:24
  57.8 28.1 %collective-permute-start.4 = (bf16[4096,128]{1,0:T(8,128)(2,1)}, bf16[4096,128]{1,0:T(8,128)(2,1)}, u32[]{:S(2)}, u32[]{:S(2)}) collective-permute-start(bf16[4096,128]{1,0:T(8,128)(2,1)} %collective-permute-done), channel_id=1, source_target_pairs={{0,4},{4,8},{8,12},{12,16},{16,20},{20,24},{24,28},{28,0},{32,60},... | collective-permute-start | bytes 3145736 | tf_op jit(solution)/shard_map/ppermute | solution.py:24
  69.1 11.4 %collective-permute-start.18 = (bf16[2,128,1024]{2,1,0:T(8,128)(2,1)S(1)}, bf16[2,128,1024]{2,1,0:T(8,128)(2,1)S(1)}, u32[]{:S(2)}, u32[]{:S(2)}) collective-permute-start(bf16[2,128,1024]{2,1,0:T(8,128)(2,1)S(1)} %pad_maximum_fusion.1.refs_5_), channel_id=1, source_target_pairs={{0,192},{64,0},{128,64},{192,128},{1,193},{65,1},{129,65},{193,129... | collective-permute-start | bytes 1572872 | tf_op jit(solution)/shard_map/ppermute | solution.py:43
  72.0 12.3 %collective-permute-start.20 = (bf16[2,128,1024]{2,1,0:T(8,128)(2,1)S(1)}, bf16[2,128,1024]{2,1,0:T(8,128)(2,1)S(1)}, u32[]{:S(2)}, u32[]{:S(2)}) collective-permute-start(bf16[2,128,1024]{2,1,0:T(8,128)(2,1)S(1)} %pad_maximum_fusion.1.refs_5_), channel_id=1, source_target_pairs={{0,64},{64,128},{128,192},{192,0},{1,65},{65,129},{129,193},{193,1... | collective-permute-start | bytes 1572872 | tf_op jit(solution)/shard_map/ppermute | solution.py:43
  73.6 17.8 %collective-permute-start.9 = (bf16[2,896,128]{2,1,0:T(8,128)(2,1)S(1)}, bf16[2,896,128]{2,1,0:T(8,128)(2,1)S(1)}, u32[]{:S(2)}, u32[]{:S(2)}) collective-permute-start(bf16[2,896,128]{2,1,0:T(8,128)(2,1)S(1)} %collective-permute-done.8.kv1), channel_id=1, source_target_pairs={{0,4},{4,8},{8,12},{12,16},{16,20},{20,24},{24,28},{28,0},{32,60},... | collective-permute-start | bytes 1376264 | tf_op jit(solution)/shard_map/ppermute | solution.py:24
  75.9 48.5 %collective-permute-start.13 = (bf16[128,1024]{1,0:T(8,128)(2,1)}, bf16[128,1024]{1,0:T(8,128)(2,1)}, u32[]{:S(2)}, u32[]{:S(2)}) collective-permute-start(bf16[128,1024]{1,0:T(8,128)(2,1)} %slice_bitcast_fusion.6), channel_id=1, source_target_pairs={{0,192},{64,0},{128,64},{192,128},{1,193},{65,1},{129,65},{193,129... | collective-permute-start | bytes 786440 | tf_op jit(solution)/shard_map/ppermute | solution.py:43
  80.5 43.8 %collective-permute-start.15 = (bf16[128,1024]{1,0:T(8,128)(2,1)}, bf16[128,1024]{1,0:T(8,128)(2,1)}, u32[]{:S(2)}, u32[]{:S(2)}) collective-permute-start(bf16[128,1024]{1,0:T(8,128)(2,1)} %slice_bitcast_fusion.5), channel_id=1, source_target_pairs={{0,64},{64,128},{128,192},{192,0},{1,65},{65,129},{129,193},{193,1... | collective-permute-start | bytes 786440 | tf_op jit(solution)/shard_map/ppermute | solution.py:43
  84.2 40.1 %collective-permute-start.19 = (bf16[128,1024]{1,0:T(8,128)(2,1)}, bf16[128,1024]{1,0:T(8,128)(2,1)}, u32[]{:S(2)}, u32[]{:S(2)}) collective-permute-start(bf16[128,1024]{1,0:T(8,128)(2,1)} %slice_bitcast_fusion.4), channel_id=1, source_target_pairs={{0,192},{64,0},{128,64},{192,128},{1,193},{65,1},{129,65},{193,129... | collective-permute-start | bytes 786440 | tf_op jit(solution)/shard_map/ppermute | solution.py:43
  85.9 17.4 %collective-permute-start.5 = (bf16[4096,128]{1,0:T(8,128)(2,1)}, bf16[4096,128]{1,0:T(8,128)(2,1)}, u32[]{:S(2)}, u32[]{:S(2)}) collective-permute-start(bf16[4096,128]{1,0:T(8,128)(2,1)} %collective-permute-done.4), channel_id=1, source_target_pairs={{0,4},{4,8},{8,12},{12,16},{16,20},{20,24},{24,28},{28,0},{32,60},... | collective-permute-start | bytes 3145736 | tf_op jit(solution)/shard_map/ppermute | solution.py:24
  91.4 19.0 %collective-permute-start.10 = (bf16[1,896,128]{2,1,0:T(8,128)(2,1)S(1)}, bf16[1,896,128]{2,1,0:T(8,128)(2,1)}, u32[]{:S(2)}, u32[]{:S(2)}) collective-permute-start(bf16[1,896,128]{2,1,0:T(8,128)(2,1)S(1)} %get-tuple-element.29), channel_id=1, source_target_pairs={{32,60},{36,32},{40,36},{44,40},{48,44},{52,48},{56,52},{60,56},{3... | collective-permute-start | bytes 688136 | tf_op jit(solution)/shard_map/ppermute | solution.py:24
  103.3 9.3 %collective-permute-start.11 = (bf16[1,896,128]{2,1,0:T(8,128)(2,1)S(1)}, bf16[1,896,128]{2,1,0:T(8,128)(2,1)S(1)}, u32[]{:S(2)}, u32[]{:S(2)}) collective-permute-start(bf16[1,896,128]{2,1,0:T(8,128)(2,1)S(1)} %get-tuple-element.30), channel_id=1, source_target_pairs={{0,36},{4,40},{8,44},{12,48},{16,52},{20,56},{24,60},{28,32},{1,37... | collective-permute-start | bytes 688136 | tf_op jit(solution)/shard_map/ppermute | solution.py:24
  110.4 10.3 %collective-permute-start.6 = (bf16[2048,128]{1,0:T(8,128)(2,1)S(1)}, bf16[2048,128]{1,0:T(8,128)(2,1)S(1)}, u32[]{:S(2)}, u32[]{:S(2)}) collective-permute-start(bf16[2048,128]{1,0:T(8,128)(2,1)S(1)} %get-tuple-element.25), channel_id=1, source_target_pairs={{32,60},{36,32},{40,36},{44,40},{48,44},{52,48},{56,52},{60,56},{3... | collective-permute-start | bytes 1572872 | tf_op jit(solution)/shard_map/ppermute | solution.py:24
  112.6 10.5 %collective-permute-start.7 = (bf16[2048,128]{1,0:T(8,128)(2,1)S(1)}, bf16[2048,128]{1,0:T(8,128)(2,1)S(1)}, u32[]{:S(2)}, u32[]{:S(2)}) collective-permute-start(bf16[2048,128]{1,0:T(8,128)(2,1)S(1)} %get-tuple-element.26), channel_id=1, source_target_pairs={{0,36},{4,40},{8,44},{12,48},{16,52},{20,56},{24,60},{28,32},{1,37... | collective-permute-start | bytes 1572872 | tf_op jit(solution)/shard_map/ppermute | solution.py:24
  120.7 9.3 %collective-permute-start.21 = (bf16[128,1024]{1,0:T(8,128)(2,1)S(1)}, bf16[128,1024]{1,0:T(8,128)(2,1)S(1)}, u32[]{:S(2)}, u32[]{:S(2)}) collective-permute-start(bf16[128,1024]{1,0:T(8,128)(2,1)S(1)} %copy-done.12), channel_id=1, source_target_pairs={{0,64},{64,128},{128,192},{192,0},{1,65},{65,129},{129,193},{193,1... | collective-permute-start | bytes 786440 | tf_op jit(solution)/shard_map/ppermute | solution.py:43
  146.8 2.0 %collective-permute-start.23 = (bf16[64,4096]{1,0:T(8,128)(2,1)S(1)}, bf16[64,4096]{1,0:T(8,128)(2,1)S(1)}, u32[]{:S(2)}, u32[]{:S(2)}) collective-permute-start(bf16[64,4096]{1,0:T(8,128)(2,1)S(1)} %slice.107), channel_id=1, source_target_pairs={{0,32},{32,0},{1,33},{33,1},{2,34},{34,2},{3,35},{35,3},{4,36},{36... | collective-permute-start | bytes 1572872 | tf_op jit(solution)/shard_map/ppermute | solution.py:43
  147.9 11.1 %collective-permute-start.22 = (bf16[3,64,4096]{2,1,0:T(8,128)(2,1)S(1)}, bf16[3,64,4096]{2,1,0:T(8,128)(2,1)S(1)}, u32[]{:S(2)}, u32[]{:S(2)}) collective-permute-start(bf16[3,64,4096]{2,1,0:T(8,128)(2,1)S(1)} %bitcast.53), channel_id=1, source_target_pairs={{0,32},{32,0},{1,33},{33,1},{2,34},{34,2},{3,35},{35,3},{4,36},{36... | collective-permute-start | bytes 4718600 | tf_op jit(solution)/shard_map/ppermute | solution.py:43
  149.0 8.4 %collective-permute-start.24 = (bf16[64,2048]{1,0:T(8,128)(2,1)S(1)}, bf16[64,2048]{1,0:T(8,128)(2,1)S(1)}, u32[]{:S(2)}, u32[]{:S(2)}) collective-permute-start(bf16[64,2048]{1,0:T(8,128)(2,1)S(1)} %get-tuple-element.27), channel_id=1, source_target_pairs={{0,1},{1,2},{2,3},{3,0},{4,5},{5,6},{6,7},{7,4},{8,9},{9,10},{10,1... | collective-permute-start | bytes 786440 | tf_op jit(solution)/shard_map/ppermute | solution.py:43
  149.5 9.4 %collective-permute-start.26 = (bf16[64,2048]{1,0:T(8,128)(2,1)S(1)}, bf16[64,2048]{1,0:T(8,128)(2,1)S(1)}, u32[]{:S(2)}, u32[]{:S(2)}) collective-permute-start(bf16[64,2048]{1,0:T(8,128)(2,1)S(1)} %get-tuple-element.28), channel_id=1, source_target_pairs={{0,3},{1,0},{2,1},{3,2},{4,7},{5,4},{6,5},{7,6},{8,11},{9,8},{10,9... | collective-permute-start | bytes 786440 | tf_op jit(solution)/shard_map/ppermute | solution.py:43
  159.3 13.1 %collective-permute-start.25 = (bf16[64,4096]{1,0:T(8,128)(2,1)S(1)}, bf16[64,4096]{1,0:T(8,128)(2,1)S(1)}, u32[]{:S(2)}, u32[]{:S(2)}) collective-permute-start(bf16[64,4096]{1,0:T(8,128)(2,1)S(1)} %get-tuple-element.23), channel_id=1, source_target_pairs={{0,1},{1,2},{2,3},{3,0},{4,5},{5,6},{6,7},{7,4},{8,9},{9,10},{10,1... | collective-permute-start | bytes 1572872 | tf_op jit(solution)/shard_map/ppermute | solution.py:43
  159.5 14.2 %collective-permute-start.27 = (bf16[64,4096]{1,0:T(8,128)(2,1)S(1)}, bf16[64,4096]{1,0:T(8,128)(2,1)S(1)}, u32[]{:S(2)}, u32[]{:S(2)}) collective-permute-start(bf16[64,4096]{1,0:T(8,128)(2,1)S(1)} %get-tuple-element.24), channel_id=1, source_target_pairs={{0,3},{1,0},{2,1},{3,2},{4,7},{5,4},{6,5},{7,6},{8,11},{9,8},{10,9... | collective-permute-start | bytes 1572872 | tf_op jit(solution)/shard_map/ppermute | solution.py:43
  (14 other events, 145.2 us)
Sparse Core Ops, SparseCore 0:
  10.0 35.6 all-gather.2
  65.6 36.0 all-gather.4
